TPU v7x, 32 devices: a whole 2x2x4 slice. The times are simulated.
32 devices in a mesh: group: 4 (over x, core), dev: 8 (over z, y).
Axes of the slice: x: 2, y: 2, z: 4, core: 2. Of those that a mesh axis runs over, the one named last changes fastest.
Arguments:
- velocity: float32 [3, 256, 128, 128], P(None, ('group', 'dev')), may hold values from -3 to 3
- viscosity: float32 [256, 128, 128], P(('group', 'dev')), may hold values from 0.04 to 0.3
- sample_idx: int32 [32, 256], P(('group', 'dev')), may hold values from 0 to 255, as said below
- assign: int32 [32, 256], P(('group', 'dev')), may hold values from 0 to 8191, as said below
- params: float32 [3670016], P(('group', 'dev')), may hold values from -0.15 to 0.15
- adam_m: float32 [3670016], P(('group', 'dev')), may hold values from -0.3 to 0.3
- adam_v: float32 [3670016], P(('group', 'dev')), may hold values from 0.0001 to 0.01
Outputs:
- velocity_next: float32 [3, 256, 128, 128], P(None, ('group', 'dev'))
- prediction: float32 [8192, 1536], P(('group', 'dev'))
- new_params: float32 [3670016], P(('group', 'dev'))
- new_m: float32 [3670016], P(('group', 'dev'))
- new_v: float32 [3670016], P(('group', 'dev'))
Inputs may be any that keep to these rules, and one draw needn't show every extreme that they name: `sample_idx`: each row holds 256 different patch numbers; 0 and the largest patch number appear in every row. `assign`: all entries together are a permutation of the 8192 learner slots; each row names exactly 8 slots of every block of 256 consecutive slots.
All inputs are finite; a program needn't handle non-finite values.
Results may differ from a plain program's by a relative error of at most 0.00011.
Values sent between devices are 32-bit elements; how exact they have to be, the bound alone decides.
No kernel may reach another device: no remote copies, remote signals or barrier semaphores. Data moves between devices by JAX's collectives and lax.ppermute only.
A program may use at most 192 MiB of HBM per device.

v0:
```python
import jax
import jax.numpy as jnp
from jax import lax
from jax.sharding import PartitionSpec as P

D = 512
H = 2048
F = 1536


time_step = 0.5
norm_epsilon = 1e-06
beta_first = 0.9
beta_second = 0.95
learn_rate = 0.01
adam_epsilon = 1e-08
adam_count = 10


def with_halo(cells, sides, width):
    for axis, dim in sides:
        count = lax.axis_size(axis)
        ends = count - 1
        head = lax.slice_in_dim(cells, 0, width, axis=dim)
        tail = lax.slice_in_dim(cells, cells.shape[dim] - width, cells.shape[dim], axis=dim)
        cells = jnp.concatenate(
            [
                lax.ppermute(tail, axis, [(i, (i + 1) % count) for i in range(ends)]),
                cells,
                lax.ppermute(head, axis, [((i + 1) % count, i) for i in range(ends)]),
            ],
            axis=dim,
        )
    return cells


def advance(extended, visc_inner):
    centre = extended[:, 1:-1]
    upper_one = extended[:, 2:]
    lower_one = extended[:, :-2]
    upper_two = jnp.roll(centre, -1, 2)
    lower_two = jnp.roll(centre, 1, 2)
    upper_three = jnp.roll(centre, -1, 3)
    lower_three = jnp.roll(centre, 1, 3)
    laplace = (
        upper_one + lower_one + upper_two + lower_two + upper_three + lower_three - 6.0 * centre
    )
    advect = 0.5 * (
        centre[0:1] * (upper_one - lower_one)
        + centre[1:2] * (upper_two - lower_two)
        + centre[2:3] * (upper_three - lower_three)
    )
    return centre + time_step * (visc_inner[None] * laplace - advect)


def patch_rows(block):
    depth = block.shape[1]
    span_y = block.shape[2] // depth
    span_z = block.shape[3] // depth
    tiles = block.reshape(3, depth, span_y, depth, span_z, depth).transpose(2, 4, 0, 1, 3, 5)
    return tiles.reshape(span_y * span_z, 3 * depth**3)


def matmul(left, right):
    return jnp.dot(left, right, precision=lax.Precision.HIGHEST, preferred_element_type=jnp.float32)


def forward(flat, inputs):
    first = F * D
    second = first + D * H
    third = second + H * D
    w_in = flat[:first].reshape(F, D)
    w_up = flat[first:second].reshape(D, H)
    w_down = flat[second:third].reshape(H, D)
    w_out = flat[third:].reshape(D, F)
    state = matmul(inputs, w_in)
    normed = state * lax.rsqrt(jnp.mean(state * state, axis=-1, keepdims=True) + norm_epsilon)
    hidden = jax.nn.gelu(matmul(normed, w_up), approximate=True)
    state = state + matmul(hidden, w_down)
    return inputs + matmul(state, w_out)


def batch_grad(flat, inputs, targets, count):

    def loss_fn(weights):
        guess = forward(weights, inputs)
        error = guess - targets
        return (0.5 * jnp.sum(error * error) / count, guess)

    loss, pull, guess = jax.vjp(loss_fn, flat, has_aux=True)
    (grad,) = pull(jnp.ones_like(loss))
    return (grad, guess)


def adam(shard, grad, moment, second):
    new_m = beta_first * moment + (1.0 - beta_first) * grad
    new_v = beta_second * second + (1.0 - beta_second) * grad * grad
    update = (
        new_m
        / (1.0 - beta_first**adam_count)
        / (jnp.sqrt(new_v / (1.0 - beta_second**adam_count)) + adam_epsilon)
    )
    return (shard - learn_rate * update, new_m, new_v)


def local(velocity, viscosity, sample_idx, assign, params, adam_m, adam_v):
    flat = lax.all_gather(params, ("group", "dev"), axis=0, tiled=True)
    stacked = jnp.concatenate([velocity, viscosity[None]], 0)
    wide = with_halo(stacked, ((("group", "dev"), 1),), 2)
    first = advance(wide[:3], wide[3, 1:-1])
    velocity_next = advance(first, viscosity)
    current = first[:, 1:-1]
    slot_count = assign.shape[1]
    target_dev = assign[0] // slot_count
    order = jnp.argsort(target_dev, stable=True)
    rows = sample_idx[0][order]
    sent_in = patch_rows(current)[rows]
    sent_out = patch_rows(velocity_next)[rows]
    sent_slot = (assign[0][order] % slot_count).astype(jnp.float32)[:, None]
    got_in, got_out, got_slot = (
        lax.all_to_all(sent_in, ("group", "dev"), split_axis=0, concat_axis=0, tiled=True),
        lax.all_to_all(sent_out, ("group", "dev"), split_axis=0, concat_axis=0, tiled=True),
        lax.all_to_all(sent_slot, ("group", "dev"), split_axis=0, concat_axis=0, tiled=True),
    )
    place = got_slot[:, 0].astype(jnp.int32)
    inputs = jnp.zeros_like(got_in).at[place].set(got_in)
    targets = jnp.zeros_like(got_out).at[place].set(got_out)
    grad, prediction = batch_grad(flat, inputs, targets, slot_count)
    grad_shard = lax.psum_scatter(grad, ("group", "dev"), scatter_dimension=0, tiled=True)
    new_params, new_m, new_v = adam(params, grad_shard, adam_m, adam_v)
    return (velocity_next, prediction, new_params, new_m, new_v)


def solution(mesh):
    placed = (
        P(None, ("group", "dev"), None, None),
        P(("group", "dev"), None, None),
        P(("group", "dev"), None),
        P(("group", "dev"), None),
        P(("group", "dev")),
        P(("group", "dev")),
        P(("group", "dev")),
    )
    return jax.shard_map(
        local,
        mesh=mesh,
        in_specs=placed,
        out_specs=(
            P(None, ("group", "dev"), None, None),
            P(("group", "dev"), None),
            P(("group", "dev")),
            P(("group", "dev")),
            P(("group", "dev")),
        ),
        check_vma=False,
    )
```

profile of v0, /device:TPU:0, one launch (start us, length us, event | category | flops | bytes accessed | tf_op | source)
XLA Modules:
  0.0 576.8 jit_solution(17558710219862887404)
XLA Ops:
  10.4 4.9 collective-permute-start
  16.7 3.2 sort.17
  22.7 6.9 %all-to-all-start = ((f32[32,8,1]{1,2,0:T(1,128)}), f32[32,8,1]{1,2,0:T(1,128)S(1)}, u32[]{:S(2)}, u32[]{:S(2)}) async-start(f32[32,8,1]{1,2,0:T(1,128)} %copy.26), calls=%async_computation | async-start | bytes 32768 | tf_op jit(solution)/shard_map/all_to_all | solution.py:123
  31.6 9.8 %collective-permute-done = f32[4,2,128,128]{3,2,1,0:T(8,128)S(1)} collective-permute-done((f32[4,2,128,128]{3,2,1,0:T(8,128)}, f32[4,2,128,128]{3,2,1,0:T(8,128)S(1)}, u32[]{:S(2)}, u32[]{:S(2)}) %collective-permute-start) | collective-permute-done | bytes 524320 | tf_op jit(solution)/shard_map/ppermute | solution.py:28
  43.9 3.1 multiply_add_fusion
  51.5 16.1 %reshape.175 = f32[3,8,16,8,16,8]{5,4,3,2,1,0:T(8,128)} reshape(f32[3,8,128,128]{3,2,1,0:T(8,128)S(1)} %get-tuple-element.26) | data formatting | bytes 3145728 | tf_op jit(solution)/shard_map/reshape | solution.py:60
  67.6 19.7 %copy.27 = f32[16,16,3,8,8,8]{1,0,5,4,3,2:T(8,128)} copy(f32[16,16,3,8,8,8]{5,1,4,0,3,2:T(8,128)} %bitcast.67) | data formatting | bytes 3145728 | tf_op jit(solution)/shard_map/transpose | solution.py:60
  87.3 8.8 %reshape.176 = f32[256,1536]{0,1:T(8,128)S(1)} reshape(f32[16,16,3,8,8,8]{1,0,5,4,3,2:T(8,128)} %copy.27) | data formatting | bytes 3145728 | tf_op jit(solution)/shard_map/reshape | solution.py:61
  98.9 6.9 %all-to-all-start.1 = ((f32[32,8,1536]{2,1,0:T(8,128)}), f32[32,8,1536]{2,1,0:T(8,128)}, u32[]{:S(2)}, u32[]{:S(2)}) async-start(f32[32,8,1536]{2,1,0:T(8,128)} %bitcast.14), calls=%async_computation.1 | async-start | bytes 3145728 | tf_op jit(solution)/shard_map/all_to_all | solution.py:121
  105.8 16.1 %reshape.178 = f32[3,8,16,8,16,8]{5,4,3,2,1,0:T(8,128)} reshape(f32[3,8,128,128]{3,2,1,0:T(8,128)S(1)} %copy-done.16) | data formatting | bytes 3145728 | tf_op jit(solution)/shard_map/reshape | solution.py:60
  121.9 18.8 %copy.29 = f32[16,16,3,8,8,8]{1,0,5,4,3,2:T(8,128)} copy(f32[16,16,3,8,8,8]{5,1,4,0,3,2:T(8,128)} %bitcast.68) | data formatting | bytes 3145728 | tf_op jit(solution)/shard_map/transpose | solution.py:60
  140.7 8.7 %reshape.179 = f32[256,1536]{0,1:T(8,128)S(1)} reshape(f32[16,16,3,8,8,8]{1,0,5,4,3,2:T(8,128)} %copy.29) | data formatting | bytes 3145728 | tf_op jit(solution)/shard_map/reshape | solution.py:61
  152.3 8.1 %all-to-all-done.1 = f32[32,8,1536]{2,1,0:T(8,128)} async-done(((f32[32,8,1536]{2,1,0:T(8,128)}), f32[32,8,1536]{2,1,0:T(8,128)}, u32[]{:S(2)}, u32[]{:S(2)}) %all-to-all-start.1) | async-done | bytes 1572896 | tf_op jit(solution)/shard_map/all_to_all | solution.py:121
  166.3 35.6 %all-to-all-done.2 = f32[32,8,1536]{2,1,0:T(8,128)S(1)} async-done(((f32[32,8,1536]{2,1,0:T(8,128)}), f32[32,8,1536]{2,1,0:T(8,128)S(1)}, u32[]{:S(2)}, u32[]{:S(2)}) %all-to-all-start.2) | async-done | bytes 1572896 | tf_op jit(solution)/shard_map/all_to_all | solution.py:122
  204.8 5.8 %fusion.44 = (f32[786432]{0:T(1024)}, f32[786432]{0:T(1024)}) fusion(f32[3670016]{0:T(1024)} %all-gather.2.cloned.1.call-done), kind=kLoop, calls=%fused_computation.106 | loop fusion | bytes 12582912 | tf_op jit(solution)/shard_map/jvp()/slice | solution.py:75
  210.6 4.6 slice.212
  215.3 5.5 multiply_reduce_fusion.1
  220.8 7.3 %fusion.45 = (f32[1048576]{0:T(1024)}, f32[1048576]{0:T(1024)}) fusion(f32[3670016]{0:T(1024)} %all-gather.2.cloned.1.call-done), kind=kLoop, calls=%fused_computation.107 | loop fusion | bytes 16777216 | tf_op jit(solution)/shard_map/jvp()/slice | solution.py:73
  228.1 4.9 slice.214
  233.0 5.0 slice.216
  240.8 5.9 %fusion.20 = f32[256,2048]{1,0:T(8,128)S(1)} fusion(f32[512,2048]{1,0:T(8,128)} %slice.214, f32[256,512]{1,0:T(8,128)} %get-tuple-element.40, f32[256]{0:T(256)S(1)} %fusion.29), kind=kOutput, calls=%fused_computation.68 | convolution fusion | flops 3221356544 | bytes 6816768 | tf_op jit(solution)/shard_map/jvp()/dot_general | solution.py:65
  246.7 4.3 convolution_add_fusion.1
  253.8 4.5 fusion.18
  258.3 3.2 fusion.17
  261.5 5.5 convolution_bitcast_fusion.1
  267.1 3.7 fusion.54
  270.8 7.0 %convolution_bitcast_fusion = f32[64,16,8,128]{3,2,1,0:T(8,128)} fusion(f32[256,512]{1,0:T(8,128)S(1)} %copy-done.11, f32[256]{0:T(256)S(1)} %fusion.29, f32[256,2048]{1,0:T(8,128)S(1)} %fusion.20, f32[256,2048]{1,0:T(8,128)S(1)} %fusion.54), kind=kOutput, calls=%fused_computation.11 | convolution fusion | flops 3231318016 | bytes 8913920 | tf_op jit(solution)/shard_map/transpose(jvp())/dot_general | solution.py:65
  277.9 5.8 %multiply_reduce_fusion = (f32[256]{0:T(256)S(1)}, f32[256,512]{1,0:T(8,128)}) fusion(f32[256,512]{1,0:T(8,128)S(1)} %copy-done.11, f32[512,2048]{1,0:T(8,128)S(1)} %copy-done.7, f32[256,2048]{1,0:T(8,128)S(1)} %fusion.20, f32[256,2048]{1,0:T(8,128)S(1)} %fusion.54), kind=kOutput, calls=%fused_computation.61 | convolution fusion | flops 3231448832 | bytes 9438208 | tf_op jit(solution)/shard_map/transpose(jvp())/dot_general | solution.py:65
  286.4 3.4 copy.31
  291.7 3.0 convolution_bitcast_fusion.2
  295.5 21.4 %pad_add_fusion = f32[3670016]{0:T(1024)} fusion(f32[786432]{0:T(1024)S(1)} %bitcast.71, f32[1048576]{0:T(1024)S(1)} %bitcast.70, f32[1048576]{0:T(1024)S(1)} %bitcast.69, f32[786432]{0:T(1024)S(1)} %reshape.180), kind=kLoop, calls=%fused_computation.6 | loop fusion | flops 11010048 | bytes 29360128 | tf_op jit(solution)/shard_map/transpose(jvp())/add_any | solution.py:72
  316.9 250.6 %all-reduce.7.cloned.1.call-done = f32[3670016]{0:T(1024)} async-done(((f32[3670016]{0:T(1024)}), f32[3670016]{0:T(1024)}) %all-reduce.7.cloned.1.call-update) | async-done | bytes 14680080
  (94 shorter events, 43.8 us)
Async XLA Ops:
  7.2 22.5 %copy-start = (s32[1,256]{1,0:T(1,128)S(1)}, s32[1,256]{1,0:T(1,128)}, u32[]{:S(2)}) copy-start(s32[1,256]{1,0:T(1,128)} %param.9) | copy-start | bytes 3076
  7.2 9.4 %copy-start.2 = (s32[1,256]{1,0:T(1,128)S(1)}, s32[1,256]{1,0:T(1,128)}, u32[]{:S(2)}) copy-start(s32[1,256]{1,0:T(1,128)} %param.10) | copy-start | bytes 3076
  7.2 197.6 %all-gather.2.cloned.1.call-start = ((), (), s32[]{:S(2)}) async-start(), calls=%async_computation.3 | async-start | bytes 15138816 | tf_op jit(solution)/shard_map/all_gather | solution.py:107
  7.9 33.5 %copy-start.9 = (f32[3,8,128,128]{3,2,1,0:T(8,128)S(1)}, f32[3,8,128,128]{3,2,1,0:T(8,128)}, u32[]{:S(2)}) copy-start(f32[3,8,128,128]{3,2,1,0:T(8,128)} %param.7) | copy-start | bytes 4718596
  7.9 33.5 %copy-start.15 = (f32[8,128,128]{2,1,0:T(8,128)S(1)}, f32[8,128,128]{2,1,0:T(8,128)}, u32[]{:S(2)}) copy-start(f32[8,128,128]{2,1,0:T(8,128)} %param.8) | copy-start | bytes 1572868
  10.4 31.0 %collective-permute-start = (f32[4,2,128,128]{3,2,1,0:T(8,128)}, f32[4,2,128,128]{3,2,1,0:T(8,128)S(1)}, u32[]{:S(2)}, u32[]{:S(2)}) collective-permute-start(f32[4,2,128,128]{3,2,1,0:T(8,128)} %get-tuple-element.24), channel_id=1, source_target_pairs={{0,1},{1,2},{2,3},{3,4},{4,5},{5,6},{6,7},{7,8},{8,9},{9,10},{10,1... | collective-permute-start | bytes 1572872 | tf_op jit(solution)/shard_map/ppermute | solution.py:28
  15.3 26.1 %collective-permute-start.1 = (f32[4,2,128,128]{3,2,1,0:T(8,128)}, f32[4,2,128,128]{3,2,1,0:T(8,128)S(1)}, u32[]{:S(2)}, u32[]{:S(2)}) collective-permute-start(f32[4,2,128,128]{3,2,1,0:T(8,128)} %get-tuple-element.25), channel_id=1, source_target_pairs={{1,0},{2,1},{3,2},{4,3},{5,4},{6,5},{7,6},{8,7},{9,8},{10,9},{11,1... | collective-permute-start | bytes 1572872 | tf_op jit(solution)/shard_map/ppermute | solution.py:30
  22.7 76.2 %all-to-all-start = ((f32[32,8,1]{1,2,0:T(1,128)}), f32[32,8,1]{1,2,0:T(1,128)S(1)}, u32[]{:S(2)}, u32[]{:S(2)}) async-start(f32[32,8,1]{1,2,0:T(1,128)} %copy.26), calls=%async_computation | async-start | bytes 32768 | tf_op jit(solution)/shard_map/all_to_all | solution.py:123
  98.9 6.9 %copy-start.16 = (f32[3,8,128,128]{3,2,1,0:T(8,128)S(1)}, f32[3,8,128,128]{3,2,1,0:T(8,128)}, u32[]{:S(2)}) copy-start(f32[3,8,128,128]{3,2,1,0:T(8,128)} %get-tuple-element.27) | copy-start | bytes 4718596
  98.9 61.5 %all-to-all-start.1 = ((f32[32,8,1536]{2,1,0:T(8,128)}), f32[32,8,1536]{2,1,0:T(8,128)}, u32[]{:S(2)}, u32[]{:S(2)}) async-start(f32[32,8,1536]{2,1,0:T(8,128)} %bitcast.14), calls=%async_computation.1 | async-start | bytes 3145728 | tf_op jit(solution)/shard_map/all_to_all | solution.py:121
  160.4 41.5 %all-to-all-start.2 = ((f32[32,8,1536]{2,1,0:T(8,128)}), f32[32,8,1536]{2,1,0:T(8,128)S(1)}, u32[]{:S(2)}, u32[]{:S(2)}) async-start(f32[32,8,1536]{2,1,0:T(8,128)} %bitcast.17), calls=%async_computation.2 | async-start | bytes 3145728 | tf_op jit(solution)/shard_map/all_to_all | solution.py:122
  163.1 404.4 %all-reduce.7.cloned.1.call-start = ((), (), s32[]{:S(2)}) async-start(), calls=%async_computation.4 | async-start | bytes 29360128
  166.3 49.0 %copy-start.4 = (f32[256,1536]{1,0:T(8,128)}, f32[256,1536]{1,0:T(8,128)S(1)}, u32[]{:S(2)}) copy-start(f32[256,1536]{1,0:T(8,128)S(1)} %scatter_custom_fusion) | copy-start | bytes 4718596
  240.8 5.9 %copy-start.3 = (f32[2048,512]{1,0:T(8,128)S(1)}, f32[2048,512]{1,0:T(8,128)}, u32[]{:S(2)}) copy-start(f32[2048,512]{1,0:T(8,128)} %slice.216) | copy-start | bytes 12582916
  240.8 5.9 %copy-start.11 = (f32[256,512]{1,0:T(8,128)S(1)}, f32[256,512]{1,0:T(8,128)}, u32[]{:S(2)}) copy-start(f32[256,512]{1,0:T(8,128)} %get-tuple-element.40) | copy-start | bytes 1572868
  246.7 4.3 copy-start.5
  251.0 2.9 copy-start.8
  253.8 4.5 copy-start.10
  261.5 5.6 copy-start.13
  270.8 7.1 %copy-start.7 = (f32[512,2048]{1,0:T(8,128)S(1)}, f32[512,2048]{1,0:T(8,128)}, u32[]{:S(2)}) copy-start(f32[512,2048]{1,0:T(8,128)} %slice.214) | copy-start | bytes 12582916
  286.4 3.5 copy-start.17
  289.9 1.4 copy-start.6
  289.9 1.5 copy-start.12
  289.9 1.7 copy-start.14
  289.9 1.8 copy-start.19
  316.9 250.6 %copy-start.18 = (f32[114688]{0:T(1024)S(1)}, f32[114688]{0:T(1024)}, u32[]{:S(2)}) copy-start(f32[114688]{0:T(1024)} %param.11) | copy-start | bytes 1376260
  316.9 250.6 %copy-start.20 = (f32[114688]{0:T(1024)S(1)}, f32[114688]{0:T(1024)}, u32[]{:S(2)}) copy-start(f32[114688]{0:T(1024)} %param.12) | copy-start | bytes 1376260
  316.9 250.6 %copy-start.21 = (f32[114688]{0:T(1024)S(1)}, f32[114688]{0:T(1024)}, u32[]{:S(2)}) copy-start(f32[114688]{0:T(1024)} %param.13) | copy-start | bytes 1376260
  316.9 252.9 %copy-start.1 = (s32[1,256]{1,0:T(1,128)S(1)}, s32[1,256]{1,0:T(1,128)}, u32[]{:S(2)}) copy-start(s32[1,256]{1,0:T(1,128)} %param.9) | copy-start | bytes 3076
Sparse Core Ops, SparseCore 0:
  10.8 144.0 all-gather.1
  317.0 250.4 all-reduce.6
where the time goes:
time: 586 us; the launch traced here: 577 us
  waiting for transfers between devices  305 us (52%)
  local copies, waits for them, and re-layouts  148 us (25%)
  matrix products  51.3 us (9%)
  other arithmetic  35.6 us (6%)
  starting transfers between devices  22.8 us (4%)
  between operations  14.8 us (3%)
    unnamed x3, waiting for transfers between devices  251 us
    dot_general x11, matrix products, matmul(): jnp.dot(left, right, precision=lax.Precision.HIGHEST, preferred_element_t...  51.3 us
    transpose x2, local copies, waits for them, and re-layouts, patch_rows(): block.reshape(3, depth, span_y, depth, span_z, depth)  38.5 us
    all_to_all x1, waiting for transfers between devices, local(): lax.all_to_all(sent_out, ('group', 'dev'), split_axis=0, concat_axis=0, t...  35.6 us
    reshape x2, local copies, waits for them, and re-layouts, patch_rows(): block.reshape(3, depth, span_y, depth, span_z, depth)  32.3 us
    add_any x1, other arithmetic, forward(): w_in = flat[:first].reshape(F, D)  21.4 us
    reshape x4, local copies, waits for them, and re-layouts, patch_rows(): return tiles.reshape(span_y * span_z, 3 * depth ** 3)  18.4 us
    slice x2, local copies, waits for them, and re-layouts, forward(): w_up = flat[first:second].reshape(D, H)  12.2 us
  transfers between devices with their start and end apart: 7, of which 4 were waited for; matrix products, arithmetic and copies ran while one was open for 21% of the time, Pallas kernels for 0%

commit v1 on v0

v1 whole, which is shorter than its diff:
```python
import functools

import jax
import jax.numpy as jnp
from jax import lax
from jax.experimental import pallas as pl
from jax.experimental.pallas import tpu as pltpu
from jax.sharding import PartitionSpec as P

time_step = 0.5
norm_epsilon = 1e-06
beta_first = 0.9
beta_second = 0.95
learn_rate = 0.01
adam_epsilon = 1e-08
adam_count = 10

AXES = ("group", "dev")
LANES = 128
GELU_A = 0.7978845608028654
GELU_B = 0.044715


def flat_ring(offset):
    count = lax.axis_size(AXES)
    if offset > 0:
        return [(i, i + 1) for i in range(count - 1)]
    return [(i + 1, i) for i in range(count - 1)]


def stepped(centre, upper, lower, nu):
    ny, nz = nu.shape
    out = []
    for c in range(3):
        mid = centre[c]
        up_y = pltpu.roll(mid, ny - 1, 0)
        lo_y = pltpu.roll(mid, 1, 0)
        up_z = pltpu.roll(mid, nz - 1, 1)
        lo_z = pltpu.roll(mid, 1, 1)
        laplace = upper[c] + lower[c] + up_y + lo_y + up_z + lo_z - 6.0 * mid
        advect = 0.5 * (
            centre[0] * (upper[c] - lower[c])
            + centre[1] * (up_y - lo_y)
            + centre[2] * (up_z - lo_z)
        )
        out.append(mid + time_step * (nu * laplace - advect))
    return out


def patch_columns(field_ref, out_ref, plane0, depth):
    ny, nz = field_ref.shape[2:]
    span = nz // depth
    per_tile = span // depth
    rows = (ny // depth) * span
    lane = lax.broadcasted_iota(jnp.int32, (1, 1, nz), 2) // depth
    row = lax.broadcasted_iota(jnp.int32, (1, span, 1), 1)

    def shear(block):
        bit = 1
        while bit < span:
            turned = pltpu.roll(block, bit * depth, 2)
            block = jnp.where((row & bit) != 0, turned, block)
            bit *= 2
        return block

    def one(t, carry):
        c = t // (depth // per_tile)
        dx = (t % (depth // per_tile)) * per_tile
        planes = [
            field_ref[c, plane0 + dx + k].reshape(ny // depth, depth, nz) for k in range(per_tile)
        ]
        block = jnp.concatenate(planes, axis=1)
        block = shear(block)
        bit = 1
        while bit < span:
            turned = pltpu.roll(block, span - bit, 1)
            block = jnp.where((lane & bit) != 0, turned, block)
            bit *= 2
        block = shear(block)
        out_ref[:, pl.ds(pl.multiple_of(t * LANES, LANES), LANES)] = block.reshape(rows, nz)
        return carry

    lax.fori_loop(0, 3 * depth // per_tile, one, 0)


def physics_kernel(vel, low, high, visc, next_out, in_out, target_out, wide, nu, first, second):
    depth = vel.shape[1]
    for c in range(3):
        wide[c, 0:2] = low[2 * c : 2 * c + 2]
        wide[c, 2 : 2 + depth] = vel[c]
        wide[c, 2 + depth : 4 + depth] = high[2 * c : 2 * c + 2]
    nu[0:1] = low[6:7]
    nu[1 : 1 + depth] = visc[...]
    nu[1 + depth : 2 + depth] = high[6:7]

    def step_one(i, carry):
        out = stepped(
            [wide[c, i + 1] for c in range(3)],
            [wide[c, i + 2] for c in range(3)],
            [wide[c, i] for c in range(3)],
            nu[i],
        )
        for c in range(3):
            first[c, i] = out[c]
        return carry

    lax.fori_loop(0, depth + 2, step_one, 0)

    def step_two(i, carry):
        out = stepped(
            [first[c, i + 1] for c in range(3)],
            [first[c, i + 2] for c in range(3)],
            [first[c, i] for c in range(3)],
            nu[i + 1],
        )
        for c in range(3):
            next_out[c, i] = out[c]
        return carry

    lax.fori_loop(0, depth, step_two, 0)
    patch_columns(first, in_out, 1, depth)
    patch_columns(next_out, target_out, 0, depth)


def physics(velocity, viscosity, low, high):
    _, depth, ny, nz = velocity.shape
    rows = (ny // depth) * (nz // depth)
    feats = 3 * depth**3
    f32 = jnp.float32
    vmem = pl.BlockSpec(memory_space=pltpu.VMEM)
    return pl.pallas_call(
        physics_kernel,
        name="physics",
        out_shape=(
            jax.ShapeDtypeStruct(velocity.shape, f32),
            jax.ShapeDtypeStruct((rows, feats), f32),
            jax.ShapeDtypeStruct((rows, feats), f32),
        ),
        in_specs=[vmem] * 4,
        out_specs=(vmem,) * 3,
        scratch_shapes=[
            pltpu.VMEM((3, depth + 4, ny, nz), f32),
            pltpu.VMEM((depth + 2, ny, nz), f32),
            pltpu.VMEM((3, depth + 2, ny, nz), f32),
            pltpu.VMEM((8, LANES), f32),
        ],
        compiler_params=pltpu.CompilerParams(vmem_limit_bytes=40 << 20),
        cost_estimate=pl.CostEstimate(
            flops=velocity.size * 120, bytes_accessed=velocity.size * 16, transcendentals=0
        ),
    )(velocity, low, high, viscosity)


NT = (((1,), (1,)), ((), ()))
TN = (((0,), (0,)), ((), ()))
NN = (((1,), (0,)), ((), ()))


def halves(value):
    top = value.astype(jnp.bfloat16)
    return top, (value - top.astype(jnp.float32)).astype(jnp.bfloat16)


def product(left, right, dims):
    dot = functools.partial(lax.dot_general, dimension_numbers=dims, preferred_element_type=jnp.float32)
    return dot(left[0], right[0]) + (dot(left[0], right[1]) + dot(left[1], right[0]))


def learn_kernel(
    shapes,
    count,
    flat_hbm,
    x_ref,
    t_ref,
    guess_out,
    grad_hbm,
    flat,
    in_hi, in_lo, up_hi, up_lo, down_hi, down_lo, out_hi, out_lo,
    pre,
    hid_hi, hid_lo,
    err_hi, err_lo,
    in_sems,
    out_sems,
):
    bases, total = [], 0
    for rows, cols in shapes:
        bases.append(total)
        total += rows * cols // LANES
    terms = [(in_hi, in_lo), (up_hi, up_lo), (down_hi, down_lo), (out_hi, out_lo)]

    def part(ref, k):
        rows, cols = shapes[k]
        return ref.at[pl.ds(bases[k], rows * cols // LANES)]

    loads = [
        pltpu.make_async_copy(part(flat_hbm, k), part(flat, k), in_sems.at[k]) for k in range(4)
    ]
    stores = [
        pltpu.make_async_copy(part(flat, k), part(grad_hbm, k), out_sems.at[k]) for k in range(4)
    ]
    for load in loads:
        load.start()

    def split(k):
        rows, cols = shapes[k]
        stride = cols // LANES
        hi, lo = terms[k]
        step = 128
        loads[k].wait()

        def some(i, carry):
            r = pl.multiple_of(i * step, step)
            for nb in range(stride):
                top, low = halves(flat[pl.ds(bases[k] + nb + r * stride, step, stride=stride), :])
                hi[pl.ds(r, step), nb * LANES : (nb + 1) * LANES] = top
                lo[pl.ds(r, step), nb * LANES : (nb + 1) * LANES] = low
            return carry

        lax.fori_loop(0, rows // step, some, 0)

    def weight(k, rows=slice(None), cols=slice(None)):
        return terms[k][0][rows, cols], terms[k][1][rows, cols]

    def keep_grad(k, row0, col0, value):
        _, cols = shapes[k]
        stride = cols // LANES
        rows, width = value.shape
        for nb in range(width // LANES):
            at = pl.ds(bases[k] + row0 * stride + col0 // LANES + nb, rows, stride=stride)
            flat[at, :] = value[:, nb * LANES : (nb + 1) * LANES]

    tokens, feats = x_ref.shape
    hidden = shapes[1][1]
    width = shapes[0][1]
    tile = 512

    split(0)
    state = product(halves(x_ref[...]), weight(0), NN)
    scale = lax.rsqrt(jnp.mean(state * state, axis=-1, keepdims=True) + norm_epsilon)
    normed = state * scale
    normed2 = halves(normed)
    split(1)
    for j in range(0, hidden, tile):
        cols = slice(j, j + tile)
        h = product(normed2, weight(1, cols=cols), NN)
        pre[:, cols] = h
        cdf = 0.5 * (1.0 + jnp.tanh(GELU_A * (h + GELU_B * (h * h * h))))
        hid_hi[:, cols], hid_lo[:, cols] = halves(h * cdf)
    split(2)
    state2 = state + product((hid_hi[...], hid_lo[...]), weight(2), NN)
    last = halves(state2)
    split(3)
    for j in range(0, feats, tile):
        cols = slice(j, j + tile)
        guess = x_ref[:, cols] + product(last, weight(3, cols=cols), NN)
        guess_out[:, cols] = guess
        error = (guess - t_ref[:, cols]) * (1.0 / count)
        err_hi[:, cols], err_lo[:, cols] = halves(error)

    for j in range(0, feats, tile):
        cols = slice(j, j + tile)
        keep_grad(3, 0, j, product(last, (err_hi[:, cols], err_lo[:, cols]), TN))
    stores[3].start()
    d_state = product((err_hi[...], err_lo[...]), weight(3), NT)
    d_last = halves(d_state)
    for j in range(0, hidden, tile):
        cols = slice(j, j + tile)
        keep_grad(2, j, 0, product((hid_hi[:, cols], hid_lo[:, cols]), d_last, TN))
        d_hid = product(d_last, weight(2, rows=cols), NT)
        h = pre[:, cols]
        tan = jnp.tanh(GELU_A * (h + GELU_B * (h * h * h)))
        slope = 0.5 * (1.0 + tan) + 0.5 * h * (1.0 - tan * tan) * (
            GELU_A * (1.0 + 3.0 * GELU_B * (h * h))
        )
        d_pre = halves(d_hid * slope)
        keep_grad(1, 0, j, product(normed2, d_pre, TN))
        hid_hi[:, cols], hid_lo[:, cols] = d_pre
    stores[2].start()
    stores[1].start()
    d_normed = product((hid_hi[...], hid_lo[...]), weight(1), NT)
    inner = jnp.mean(d_normed * normed, axis=-1, keepdims=True)
    d_state = d_state + scale * (d_normed - normed * inner)
    d_first = halves(d_state)
    for j in range(0, feats, tile):
        cols = slice(j, j + tile)
        keep_grad(0, j, 0, product(halves(x_ref[:, cols]), d_first, TN))
    stores[0].start()
    for store in stores:
        store.wait()


def learn(flat, inputs, targets, shapes, count):
    f32, bf16 = jnp.float32, jnp.bfloat16
    tokens, feats = inputs.shape
    hidden = shapes[1][1]
    vmem = pl.BlockSpec(memory_space=pltpu.VMEM)
    hbm = pl.BlockSpec(memory_space=pl.ANY)
    scratch = [pltpu.VMEM(flat.shape, f32)]
    for shape in shapes:
        scratch += [pltpu.VMEM(shape, bf16)] * 2
    scratch += [pltpu.VMEM((tokens, hidden), f32)]
    scratch += [pltpu.VMEM((tokens, hidden), bf16)] * 2
    scratch += [pltpu.VMEM((tokens, feats), bf16)] * 2
    scratch += [pltpu.SemaphoreType.DMA((4,)), pltpu.SemaphoreType.DMA((4,))]
    return pl.pallas_call(
        functools.partial(learn_kernel, shapes, count),
        name="learn",
        out_shape=(
            jax.ShapeDtypeStruct((tokens, feats), f32),
            jax.ShapeDtypeStruct(flat.shape, f32),
        ),
        in_specs=[hbm, vmem, vmem],
        out_specs=(vmem, hbm),
        scratch_shapes=scratch,
        compiler_params=pltpu.CompilerParams(vmem_limit_bytes=62 << 20),
        cost_estimate=pl.CostEstimate(
            flops=tokens * flat.size * 18, bytes_accessed=flat.size * 8, transcendentals=tokens * hidden * 2
        ),
    )(flat, inputs, targets)


def adam(shard, grad, moment, second):
    new_m = beta_first * moment + (1.0 - beta_first) * grad
    new_v = beta_second * second + (1.0 - beta_second) * grad * grad
    update = (
        new_m
        / (1.0 - beta_first**adam_count)
        / (jnp.sqrt(new_v / (1.0 - beta_second**adam_count)) + adam_epsilon)
    )
    return (shard - learn_rate * update, new_m, new_v)


def gather_params(params):
    return lax.all_gather(params.reshape(-1, LANES), AXES, axis=0, tiled=True)


def scatter_grad(grad):
    return lax.psum_scatter(grad.reshape(-1), AXES, scatter_dimension=0, tiled=True)


def local(shapes, velocity, viscosity, sample_idx, assign, params, adam_m, adam_v):
    flat = gather_params(params)
    _, depth, ny, nz = velocity.shape
    planes = lambda a, b: jnp.concatenate(
        [velocity[:, a : a + 2].reshape(6, ny, nz), viscosity[b : b + 1]], 0
    )
    low = lax.ppermute(planes(depth - 2, depth - 1), AXES, flat_ring(1))
    high = lax.ppermute(planes(0, 0), AXES, flat_ring(-1))

    slots = assign.shape[1]
    owner = assign[0] // slots
    order = jnp.argsort(owner, stable=True)
    span = nz // depth
    patch = sample_idx[0][order]
    rows = patch - patch % span + (span - patch % span) % span
    place = lax.all_to_all(
        (assign[0][order] % slots)[:, None], AXES, split_axis=0, concat_axis=0, tiled=True
    )[:, 0]
    source = jnp.zeros((slots,), jnp.int32).at[place].set(jnp.arange(slots, dtype=jnp.int32))

    velocity_next, inputs, targets = physics(velocity, viscosity, low, high)
    guess, grad = learn(flat, inputs, targets, shapes, slots)
    got = lax.all_to_all(guess[rows], AXES, split_axis=0, concat_axis=0, tiled=True)
    prediction = got[source]
    new_params, new_m, new_v = adam(params, scatter_grad(grad), adam_m, adam_v)
    return (velocity_next, prediction, new_params, new_m, new_v)


def solution(mesh):
    block = P(AXES)
    slab = P(None, AXES, None, None)

    def step(velocity, viscosity, sample_idx, assign, params, adam_m, adam_v):
        devices = mesh.size
        depth = velocity.shape[1] // devices
        feats = 3 * depth**3
        wide = 512
        hidden = (params.size - 2 * feats * wide) // (2 * wide)
        assert 2 * wide * (feats + hidden) == params.size
        assert sample_idx.shape[1] * depth**2 == velocity.shape[2] * velocity.shape[3]
        shapes = ((feats, wide), (wide, hidden), (hidden, wide), (wide, feats))
        return jax.shard_map(
            functools.partial(local, shapes),
            mesh=mesh,
            in_specs=(slab, block, block, block, block, block, block),
            out_specs=(slab, block, block, block, block),
            check_vma=False,
        )(velocity, viscosity, sample_idx, assign, params, adam_m, adam_v)

    return step
```

time: 586 us -> 453 us (0.77); the launches traced: 577 us -> 453 us
  local copies, waits for them, and re-layouts: 148 us -> 15.8 us
  matrix products: 51.3 us -> 0 us
  Pallas kernels: 0 us -> 49.4 us
  waiting for transfers between devices: 305 us -> 354 us
  other arithmetic: 35.6 us -> 6.9 us
  starting transfers between devices: 22.8 us -> 12.4 us
    all_gather x1, waiting for transfers between devices: 0.01 us -> 68.9 us  [gather_params(): return lax.all_gather(params.reshape(-1, LANES), AXES, axis=0, tiled=True)]
    reshape x8 -> x0, local copies, waits for them, and re-layouts: 56.2 us -> none  [the longest x2 32.3 us: patch_rows(): block.reshape(3, depth, span_y, depth, span_z, depth)]
    dot_general x11 -> x0, matrix products: 51.3 us -> none  [matmul(): jnp.dot(left, right, precision=lax.Precision.HIGHEST, preferred_element_t...]
    pallas_call x0 -> x2, Pallas kernels: none -> 49.4 us  [the longest x1 30.6 us: learn(): pl.pallas_call(functools.partial(learn_kernel, shapes, count), name='lear...]
    unnamed x3, waiting for transfers between devices: 251 us -> 208 us
    transpose x2 -> x0, local copies, waits for them, and re-layouts: 38.5 us -> none  [patch_rows(): block.reshape(3, depth, span_y, depth, span_z, depth)]
    slice x12 -> x2, local copies, waits for them, and re-layouts: 31 us -> 2.2 us  [the longest x1 1.32 us: local(): velocity[:, a:a + 2].reshape(6, ny, nz)]
    add_any x1 -> x0, other arithmetic: 21.4 us -> none  [forward(): w_in = flat[:first].reshape(F, D)]
  transfers between devices with their start and end apart: 7 -> 6, of which waited for: 4 -> 5; matrix products, arithmetic and copies ran while one was open for 21% -> 4% of each run, Pallas kernels for 0% -> 4%
where the time goes in v1:
time: 453 us
  waiting for transfers between devices  354 us (78%)
  Pallas kernels  49.4 us (11%)
  local copies, waits for them, and re-layouts  15.8 us (3%)
  between operations  14.2 us (3%)
  starting transfers between devices  12.4 us (3%)
  other arithmetic  6.9 us (2%)
    unnamed x3, waiting for transfers between devices  208 us
    all_gather x1, waiting for transfers between devices, gather_params(): return lax.all_gather(params.reshape(-1, LANES), AXES, axis=0, tiled=True)  68.9 us
    all_to_all x1, waiting for transfers between devices, local(): lax.all_to_all(guess[rows], AXES, split_axis=0, concat_axis=0, tiled=True)  53 us
    pallas_call x1, Pallas kernels, learn(): pl.pallas_call(functools.partial(learn_kernel, shapes, count), name='lear...  30.6 us
    ppermute x1, waiting for transfers between devices, local(): low = lax.ppermute(planes(depth - 2, depth - 1), AXES, flat_ring(1))  21.5 us
    pallas_call x1, Pallas kernels, physics(): pl.pallas_call(physics_kernel, name='physics', out_shape=(jax.ShapeDtypeS...  18.8 us
  transfers between devices with their start and end apart: 6, of which 5 were waited for; matrix products, arithmetic and copies ran while one was open for 4% of the time, Pallas kernels for 4%

profile of v1, /device:TPU:0, one launch (start us, length us, event | category | flops | bytes accessed | tf_op | source)
XLA Modules:
  0.0 452.6 jit_solution(11062971111131414544)
XLA Ops:
  7.2 0.0 all-gather.2.cloned.1.call-start
  7.2 0.7 all-gather.2.cloned.1.call-update
  7.9 0.0 all-reduce.3.cloned.1.call-start
  8.0 0.9 fusion.9
  8.9 1.3 fusion.8
  10.2 4.9 %collective-permute-start = (f32[7,128,128]{2,1,0:T(8,128)S(1)}, f32[7,128,128]{2,1,0:T(8,128)S(1)}, u32[]{:S(2)}, u32[]{:S(2)}) collective-permute-start(f32[7,128,128]{2,1,0:T(8,128)S(1)} %pad_maximum_fusion), channel_id=1, source_target_pairs={{0,1},{1,2},{2,3},{3,4},{4,5},{5,6},{6,7},{7,8},{8,9},{9,10},{10,1... | collective-permute-start | bytes 1376264 | tf_op jit(solution)/shard_map/ppermute | solution.py:347
  15.2 1.3 collective-permute-start.1
  16.5 21.5 %collective-permute-done.low = f32[7,128,128]{2,1,0:T(8,128)S(1)} collective-permute-done((f32[7,128,128]{2,1,0:T(8,128)S(1)}, f32[7,128,128]{2,1,0:T(8,128)S(1)}, u32[]{:S(2)}, u32[]{:S(2)}) %collective-permute-start) | collective-permute-done | bytes 458784 | tf_op jit(solution)/shard_map/ppermute | solution.py:347
  38.0 18.8 %physics.1 = (f32[3,8,128,128]{3,2,1,0:T(8,128)}, f32[256,1536]{1,0:T(8,128)S(1)}, f32[256,1536]{1,0:T(8,128)S(1)}) custom-call(f32[3,8,128,128]{3,2,1,0:T(8,128)S(1)} %copy-done.1, f32[7,128,128]{2,1,0:T(8,128)S(1)} %collective-permute-done.low, f32[7,128,128]{2,1,0:T(8,128)S(1)} %collective-permute-done.1.high, f32[8,128,128]{2,1,0:T(8,128)S(1)} %copy-done.2), custom_call_target="tpu_custom_call" | custom-call | flops 47185920 | bytes 6291456 | tf_op jit(solution)/shard_map/physics/pallas_call | solution.py:131
  56.8 1.1 copy-done.3
  57.9 1.1 copy-done.4
  59.1 68.9 %all-gather.2.cloned.1.call-done.flat_hbm = f32[28672,128]{1,0:T(8,128)} async-done(((f32[896,128]{1,0:T(8,128)}), f32[28672,128]{1,0:T(8,128)}) %all-gather.2.cloned.1.call-update) | async-done | bytes 14680080 | tf_op jit(solution)/shard_map/all_gather | solution.py:334
  128.0 30.6 %learn.1 = (f32[256,1536]{1,0:T(8,128)}, f32[28672,128]{1,0:T(8,128)}) custom-call(f32[28672,128]{1,0:T(8,128)} %all-gather.2.cloned.1.call-done.flat_hbm, f32[256,1536]{1,0:T(8,128)} %copy-done.3, f32[256,1536]{1,0:T(8,128)} %copy-done.4), custom_call_target="tpu_custom_call" | custom-call | flops 16911433728 | bytes 29360128 | tf_op jit(solution)/shard_map/learn/pallas_call | solution.py:305
  158.6 0.0 all-reduce.3.cloned.1.call-update
  158.6 0.6 copy-done.5
  159.2 3.2 sort.17
  162.4 1.9 gather_fusion.2
  164.4 0.1 gather.20
  164.5 0.6 add_select_fusion
  165.1 3.2 all-to-all-start.1
  168.3 1.9 gather_fusion
  170.3 2.3 gather_fusion.1
  172.6 2.7 all-to-all-done.1
  175.4 2.9 all-to-all-start
  178.3 0.5 broadcast.195
  178.8 0.7 reduce.3
  179.5 0.1 all_to_all.18
  179.6 1.4 scatter_custom_fusion
  181.0 53.0 %all-to-all-done = f32[32,8,1536]{2,1,0:T(8,128)S(1)} async-done(((f32[32,8,1536]{2,1,0:T(8,128)}), f32[32,8,1536]{2,1,0:T(8,128)S(1)}, u32[]{:S(2)}, u32[]{:S(2)}) %all-to-all-start) | async-done | bytes 1572896 | tf_op jit(solution)/shard_map/all_to_all | solution.py:363
  234.1 2.3 gather_fusion.3
  236.4 207.0 %all-reduce.3.cloned.1.call-done = f32[3670016]{0:T(1024)} async-done(((f32[3670016]{0:T(1024)}), f32[3670016]{0:T(1024)}) %all-reduce.3.cloned.1.call-update) | async-done | bytes 14680080
  443.4 2.3 multiply_subtract_fusion
  (30 shorter events, 0.2 us)
Async XLA Ops:
  7.2 161.1 %copy-start = (s32[1,256]{1,0:T(1,128)S(1)}, s32[1,256]{1,0:T(1,128)}, u32[]{:S(2)}) copy-start(s32[1,256]{1,0:T(1,128)} %param.9) | copy-start | bytes 3076
  7.2 120.8 %all-gather.2.cloned.1.call-start = ((), (), s32[]{:S(2)}) async-start(), calls=%async_computation.2 | async-start | bytes 15138816 | tf_op jit(solution)/shard_map/all_gather | solution.py:334
  7.9 435.5 %all-reduce.3.cloned.1.call-start = ((), (), s32[]{:S(2)}) async-start(), calls=%async_computation.3 | async-start | bytes 29360128
  8.8 29.2 %copy-start.1 = (f32[3,8,128,128]{3,2,1,0:T(8,128)S(1)}, f32[3,8,128,128]{3,2,1,0:T(8,128)}, u32[]{:S(2)}) copy-start(f32[3,8,128,128]{3,2,1,0:T(8,128)} %vel.1) | copy-start | bytes 4718596
  8.9 29.1 %copy-start.2 = (f32[8,128,128]{2,1,0:T(8,128)S(1)}, f32[8,128,128]{2,1,0:T(8,128)}, u32[]{:S(2)}) copy-start(f32[8,128,128]{2,1,0:T(8,128)} %visc.1) | copy-start | bytes 1572868
  10.2 27.8 %collective-permute-start = (f32[7,128,128]{2,1,0:T(8,128)S(1)}, f32[7,128,128]{2,1,0:T(8,128)S(1)}, u32[]{:S(2)}, u32[]{:S(2)}) collective-permute-start(f32[7,128,128]{2,1,0:T(8,128)S(1)} %pad_maximum_fusion), channel_id=1, source_target_pairs={{0,1},{1,2},{2,3},{3,4},{4,5},{5,6},{6,7},{7,8},{8,9},{9,10},{10,1... | collective-permute-start | bytes 1376264 | tf_op jit(solution)/shard_map/ppermute | solution.py:347
  15.2 22.8 %collective-permute-start.1 = (f32[7,128,128]{2,1,0:T(8,128)S(1)}, f32[7,128,128]{2,1,0:T(8,128)S(1)}, u32[]{:S(2)}, u32[]{:S(2)}) collective-permute-start(f32[7,128,128]{2,1,0:T(8,128)S(1)} %pad_maximum_fusion.1), channel_id=1, source_target_pairs={{1,0},{2,1},{3,2},{4,3},{5,4},{6,5},{7,6},{8,7},{9,8},{10,9},{11,1... | collective-permute-start | bytes 1376264 | tf_op jit(solution)/shard_map/ppermute | solution.py:348
  56.8 1.1 copy-start.3
  57.9 1.1 copy-start.4
  158.6 0.7 copy-start.5
  158.6 11.7 %copy-start.6 = (f32[256,1536]{1,0:T(8,128)S(1)}, f32[256,1536]{1,0:T(8,128)}, u32[]{:S(2)}) copy-start(f32[256,1536]{1,0:T(8,128)} %get-tuple-element.14) | copy-start | bytes 4718596
  165.1 10.3 %all-to-all-start.1 = ((s32[32,8,1]{1,2,0:T(1,128)}), s32[32,8,1]{1,2,0:T(1,128)S(1)}, u32[]{:S(2)}, u32[]{:S(2)}) async-start(s32[32,8,1]{1,2,0:T(1,128)} %bitcast.9), calls=%async_computation.1 | async-start | bytes 32768 | tf_op jit(solution)/shard_map/all_to_all | solution.py:356
  175.4 58.7 %all-to-all-start = ((f32[32,8,1536]{2,1,0:T(8,128)}), f32[32,8,1536]{2,1,0:T(8,128)S(1)}, u32[]{:S(2)}, u32[]{:S(2)}) async-start(f32[32,8,1536]{2,1,0:T(8,128)} %bitcast.7), calls=%async_computation | async-start | bytes 3145728 | tf_op jit(solution)/shard_map/all_to_all | solution.py:363
  234.1 209.4 %copy-start.7 = (f32[114688]{0:T(1024)S(1)}, f32[114688]{0:T(1024)}, u32[]{:S(2)}) copy-start(f32[114688]{0:T(1024)} %param.11) | copy-start | bytes 1376260
  234.1 209.4 %copy-start.8 = (f32[114688]{0:T(1024)S(1)}, f32[114688]{0:T(1024)}, u32[]{:S(2)}) copy-start(f32[114688]{0:T(1024)} %param.12) | copy-start | bytes 1376260
  234.1 209.4 %copy-start.9 = (f32[114688]{0:T(1024)S(1)}, f32[114688]{0:T(1024)}, u32[]{:S(2)}) copy-start(f32[114688]{0:T(1024)} %param.13) | copy-start | bytes 1376260
Sparse Core Ops, SparseCore 0:
  10.8 117.0 all-gather.1
  158.7 284.6 all-reduce.2

commit v2 on v1

--- a/solution.py
+++ b/solution.py
@@ -1,7 +1,9 @@
 import functools
+import itertools
 
 import jax
 import jax.numpy as jnp
+import numpy as np
 from jax import lax
 from jax.experimental import pallas as pl
 from jax.experimental.pallas import tpu as pltpu
@@ -169,11 +171,30 @@
 def learn_kernel(
     shapes,
     count,
-    flat_hbm,
+    n_in,
+    n_out,
+    rows_in,
+    rows_out,
     x_ref,
     t_ref,
+    *refs,
+):
+    pieces_in, refs = refs[:n_in], refs[n_in:]
+    guess_out, refs = refs[0], refs[1:]
+    pieces_out, refs = refs[:n_out], refs[n_out:]
+    learn_body(shapes, count, rows_in, rows_out, x_ref, t_ref, pieces_in, guess_out, pieces_out, *refs)
+
+
+def learn_body(
+    shapes,
+    count,
+    rows_in,
+    rows_out,
+    x_ref,
+    t_ref,
+    pieces_in,
     guess_out,
-    grad_hbm,
+    pieces_out,
     flat,
     in_hi, in_lo, up_hi, up_lo, down_hi, down_lo, out_hi, out_lo,
     pre,
@@ -188,25 +209,32 @@
         total += rows * cols // LANES
     terms = [(in_hi, in_lo), (up_hi, up_lo), (down_hi, down_lo), (out_hi, out_lo)]
 
-    def part(ref, k):
-        rows, cols = shapes[k]
-        return ref.at[pl.ds(bases[k], rows * cols // LANES)]
-
-    loads = [
-        pltpu.make_async_copy(part(flat_hbm, k), part(flat, k), in_sems.at[k]) for k in range(4)
-    ]
-    stores = [
-        pltpu.make_async_copy(part(flat, k), part(grad_hbm, k), out_sems.at[k]) for k in range(4)
-    ]
+    def at_rows(table, i, rows):
+        return flat.at[pl.ds(pl.multiple_of(table[i], 8), rows)]
+
+    loads, stores = [], []
+    for ref in pieces_in:
+        for b in range(ref.shape[0]):
+            i = len(loads)
+            loads.append(
+                pltpu.make_async_copy(ref.at[b], at_rows(rows_in, i, ref.shape[1]), in_sems.at[i])
+            )
+    for ref in pieces_out:
+        for b in range(ref.shape[0]):
+            i = len(stores)
+            stores.append(
+                pltpu.make_async_copy(at_rows(rows_out, i, ref.shape[1]), ref.at[b], out_sems.at[i])
+            )
     for load in loads:
         load.start()
+    for load in loads:
+        load.wait()
 
     def split(k):
         rows, cols = shapes[k]
         stride = cols // LANES
         hi, lo = terms[k]
         step = 128
-        loads[k].wait()
 
         def some(i, carry):
             r = pl.multiple_of(i * step, step)
@@ -260,7 +288,6 @@
     for j in range(0, feats, tile):
         cols = slice(j, j + tile)
         keep_grad(3, 0, j, product(last, (err_hi[:, cols], err_lo[:, cols]), TN))
-    stores[3].start()
     d_state = product((err_hi[...], err_lo[...]), weight(3), NT)
     d_last = halves(d_state)
     for j in range(0, hidden, tile):
@@ -275,8 +302,6 @@
         d_pre = halves(d_hid * slope)
         keep_grad(1, 0, j, product(normed2, d_pre, TN))
         hid_hi[:, cols], hid_lo[:, cols] = d_pre
-    stores[2].start()
-    stores[1].start()
     d_normed = product((hid_hi[...], hid_lo[...]), weight(1), NT)
     inner = jnp.mean(d_normed * normed, axis=-1, keepdims=True)
     d_state = d_state + scale * (d_normed - normed * inner)
@@ -284,39 +309,41 @@
     for j in range(0, feats, tile):
         cols = slice(j, j + tile)
         keep_grad(0, j, 0, product(halves(x_ref[:, cols]), d_first, TN))
-    stores[0].start()
+    for store in stores:
+        store.start()
     for store in stores:
         store.wait()
 
 
-def learn(flat, inputs, targets, shapes, count):
+def learn(pieces, rows_in, out_shapes, rows_out, inputs, targets, shapes, count):
     f32, bf16 = jnp.float32, jnp.bfloat16
     tokens, feats = inputs.shape
     hidden = shapes[1][1]
+    total = sum(rows * cols for rows, cols in shapes)
     vmem = pl.BlockSpec(memory_space=pltpu.VMEM)
+    smem = pl.BlockSpec(memory_space=pltpu.SMEM)
     hbm = pl.BlockSpec(memory_space=pl.ANY)
-    scratch = [pltpu.VMEM(flat.shape, f32)]
+    scratch = [pltpu.VMEM((total // LANES, LANES), f32)]
     for shape in shapes:
         scratch += [pltpu.VMEM(shape, bf16)] * 2
     scratch += [pltpu.VMEM((tokens, hidden), f32)]
     scratch += [pltpu.VMEM((tokens, hidden), bf16)] * 2
     scratch += [pltpu.VMEM((tokens, feats), bf16)] * 2
-    scratch += [pltpu.SemaphoreType.DMA((4,)), pltpu.SemaphoreType.DMA((4,))]
-    return pl.pallas_call(
-        functools.partial(learn_kernel, shapes, count),
+    scratch += [pltpu.SemaphoreType.DMA(rows_in.shape), pltpu.SemaphoreType.DMA(rows_out.shape)]
+    guess, *grads = pl.pallas_call(
+        functools.partial(learn_kernel, shapes, count, len(pieces), len(out_shapes)),
         name="learn",
-        out_shape=(
-            jax.ShapeDtypeStruct((tokens, feats), f32),
-            jax.ShapeDtypeStruct(flat.shape, f32),
-        ),
-        in_specs=[hbm, vmem, vmem],
-        out_specs=(vmem, hbm),
+        out_shape=(jax.ShapeDtypeStruct((tokens, feats), f32),)
+        + tuple(jax.ShapeDtypeStruct(shape, f32) for shape in out_shapes),
+        in_specs=[smem, smem, vmem, vmem] + [hbm] * len(pieces),
+        out_specs=(vmem,) + (hbm,) * len(out_shapes),
         scratch_shapes=scratch,
         compiler_params=pltpu.CompilerParams(vmem_limit_bytes=62 << 20),
         cost_estimate=pl.CostEstimate(
-            flops=tokens * flat.size * 18, bytes_accessed=flat.size * 8, transcendentals=tokens * hidden * 2
+            flops=tokens * total * 18, bytes_accessed=total * 8, transcendentals=tokens * hidden * 2
         ),
-    )(flat, inputs, targets)
+    )(rows_in, rows_out, inputs, targets, *pieces)
+    return guess, grads
 
 
 def adam(shard, grad, moment, second):
@@ -330,16 +357,136 @@
     return (shard - learn_rate * update, new_m, new_v)
 
 
-def gather_params(params):
-    return lax.all_gather(params.reshape(-1, LANES), AXES, axis=0, tiled=True)
-
-
-def scatter_grad(grad):
-    return lax.psum_scatter(grad.reshape(-1), AXES, scatter_dimension=0, tiled=True)
-
-
-def local(shapes, velocity, viscosity, sample_idx, assign, params, adam_m, adam_v):
-    flat = gather_params(params)
+def moved(value, axes, move):
+    sizes = (2, 2, 4, 2)
+    pairs = []
+    for here in itertools.product(*(range(n) for n in sizes)):
+        there = move(*here)
+        if there is not None:
+            pairs.append(tuple(functools.reduce(lambda a, b: a * b[0] + b[1], zip(sizes, p), 0) for p in (here, there)))
+    return lax.ppermute(value, axes, pairs)
+
+
+def core(x, c, z, y):
+    return (x, 1 - c, z, y)
+
+
+def near(x, c, z, y):
+    return (x, c, z, 1 - y) if c == 0 else (1 - x, c, z, y)
+
+
+def far(x, c, z, y):
+    return (1 - x, c, z, y) if c == 0 else (x, c, z, 1 - y)
+
+
+def pair(x, c, z, y):
+    return (x, c, z ^ 1, y)
+
+
+def middle(x, c, z, y):
+    return (x, c, 3 - z, y) if z in (1, 2) else None
+
+
+def outward(x, c, z, y):
+    return (x, c, 0 if z == 1 else 3, y) if z in (1, 2) else None
+
+
+def inward(x, c, z, y):
+    return (x, c, 1 if z == 0 else 2, y) if z in (0, 3) else None
+
+
+def place(axes):
+    g, d = lax.axis_index(axes[0]), lax.axis_index(axes[1])
+    return g // 2, g % 2, d // 2, d % 2
+
+
+def block_rows(axes, rows, half, order, dp, dq, owner):
+    x, _, z, y = place(axes)
+    step_x, step_y = (dp, dq) if half == 0 else (dq, dp)
+    low = z < 2
+    far_z = (z, z ^ 1, jnp.where(low, 2, 1), jnp.where(low, 3, 0))[order]
+    shard = (((x ^ step_x) * 2 + owner) * 4 + far_z) * 2 + (y ^ step_y)
+    return shard * rows + half * (rows // 2)
+
+
+def piece_rows(axes, rows, order, mine, dp, dq):
+    c = lax.axis_index(axes[0]) % 2
+    at = [block_rows(axes, rows, half, order, dp, dq, owner) for half in (0, 1) for owner in (0, 1)]
+    first = (c == 0) == mine
+    return [jnp.where(first, at[o], at[2 + o]) for o in (0, 1)]
+
+
+def gather_pieces(params, axes):
+    shard = params.reshape(-1, LANES)
+    rows = shard.shape[0]
+    c = lax.axis_index(axes[0]) % 2
+    parts = shard.reshape(2, rows // 2, LANES)
+    mine = lax.dynamic_index_in_dim(parts, c, 0, False)
+    got = moved(lax.dynamic_index_in_dim(parts, 1 - c, 0, False), axes, core)
+    own = jnp.where(c == 0, jnp.stack([mine, got]), jnp.stack([got, mine]))
+    one = moved(own, axes, pair)
+    two_mid = moved(own, axes, middle)
+    two_end = moved(two_mid, axes, outward)
+    three_mid = moved(one, axes, middle)
+    three_end = moved(three_mid, axes, outward)
+    pieces, table = [], []
+    for order, block in enumerate((own, one, two_mid + two_end, three_mid + three_end)):
+        q = moved(block, axes, near)
+        p = moved(block, axes, far)
+        both = moved(q, axes, far)
+        for value, dp, dq in ((block, 0, 0), (q, 0, 1), (p, 1, 0), (both, 1, 1)):
+            pieces += [value, moved(value, axes, core)]
+            table += piece_rows(axes, rows, order, True, dp, dq)
+            table += piece_rows(axes, rows, order, False, dp, dq)
+    return pieces, jnp.stack(table)
+
+
+def scatter_rows(rows, axes):
+    table = []
+    for mine in (True, False):
+        for order in (3, 2, 1, 0):
+            for dp, dq in ((1, 1), (1, 0), (0, 1), (0, 0)):
+                table += piece_rows(axes, rows, order, mine, dp, dq)
+    return [(8, rows // 2, LANES)] * 8, jnp.stack(table)
+
+
+def scatter_pieces(grads, axes):
+    grads = [g.reshape(4, 2, g.shape[1], LANES) for g in grads]
+    parts = []
+    for mine, other in zip(grads[:4], grads[4:]):
+        got = moved(other, axes, core)
+        p = moved(mine[0:2] + got[0:2], axes, far)
+        q = moved((mine[2] + got[2]) + p[0], axes, near)
+        parts.append((mine[3] + got[3]) + p[1] + q)
+    three = moved(parts[0], axes, inward)
+    three = moved(parts[0] + three, axes, middle)
+    two = moved(parts[1], axes, inward)
+    two = moved(parts[1] + two, axes, middle)
+    one = moved(parts[2] + three, axes, pair)
+    total = parts[3] + one + two
+    c = lax.axis_index(axes[0]) % 2
+    keep = lax.dynamic_index_in_dim(total, c, 0, False)
+    got = moved(lax.dynamic_index_in_dim(total, 1 - c, 0, False), axes, core)
+    return jnp.where(c == 0, jnp.concatenate([keep, got]), jnp.concatenate([got, keep])).reshape(-1)
+
+
+def gather_flat(params, axes):
+    flat = lax.all_gather(params.reshape(-1, LANES), axes, axis=0, tiled=True)
+    return [flat[None]], jnp.zeros((1,), jnp.int32)
+
+
+def flat_rows(rows, axes):
+    return [(1, rows * lax.axis_size(axes), LANES)], jnp.zeros((1,), jnp.int32)
+
+
+def scatter_flat(grads, axes):
+    return lax.psum_scatter(grads[0].reshape(-1), axes, scatter_dimension=0, tiled=True)
+
+
+def local(shapes, exchange, velocity, viscosity, sample_idx, assign, params, adam_m, adam_v):
+    gather, result_rows, scatter = exchange
+    pieces, rows_in = gather(params, AXES)
+    out_shapes, rows_out = result_rows(params.size // LANES, AXES)
     _, depth, ny, nz = velocity.shape
     planes = lambda a, b: jnp.concatenate(
         [velocity[:, a : a + 2].reshape(6, ny, nz), viscosity[b : b + 1]], 0
@@ -353,21 +500,34 @@
     span = nz // depth
     patch = sample_idx[0][order]
     rows = patch - patch % span + (span - patch % span) % span
-    place = lax.all_to_all(
+    slot = lax.all_to_all(
         (assign[0][order] % slots)[:, None], AXES, split_axis=0, concat_axis=0, tiled=True
     )[:, 0]
-    source = jnp.zeros((slots,), jnp.int32).at[place].set(jnp.arange(slots, dtype=jnp.int32))
+    source = jnp.zeros((slots,), jnp.int32).at[slot].set(jnp.arange(slots, dtype=jnp.int32))
 
     velocity_next, inputs, targets = physics(velocity, viscosity, low, high)
-    guess, grad = learn(flat, inputs, targets, shapes, slots)
+    guess, grads = learn(pieces, rows_in, out_shapes, rows_out, inputs, targets, shapes, slots)
     got = lax.all_to_all(guess[rows], AXES, split_axis=0, concat_axis=0, tiled=True)
     prediction = got[source]
-    new_params, new_m, new_v = adam(params, scatter_grad(grad), adam_m, adam_v)
+    new_params, new_m, new_v = adam(params, scatter(grads, AXES), adam_m, adam_v)
     return (velocity_next, prediction, new_params, new_m, new_v)
+
+
+def chip_lines(mesh):
+    if tuple(mesh.devices.shape) != (4, 8):
+        return False
+    return all(
+        tuple(d.coords) == (g // 2, i % 2, i // 2) and d.core_on_chip == g % 2
+        for (g, i), d in np.ndenumerate(mesh.devices)
+    )
 
 
 def solution(mesh):
     block = P(AXES)
+    if chip_lines(mesh):
+        exchange = (gather_pieces, scatter_rows, scatter_pieces)
+    else:
+        exchange = (gather_flat, flat_rows, scatter_flat)
     slab = P(None, AXES, None, None)
 
     def step(velocity, viscosity, sample_idx, assign, params, adam_m, adam_v):
@@ -380,7 +540,7 @@
         assert sample_idx.shape[1] * depth**2 == velocity.shape[2] * velocity.shape[3]
         shapes = ((feats, wide), (wide, hidden), (hidden, wide), (wide, feats))
         return jax.shard_map(
-            functools.partial(local, shapes),
+            functools.partial(local, shapes, exchange),
             mesh=mesh,
             in_specs=(slab, block, block, block, block, block, block),
             out_specs=(slab, block, block, block, block),

time: 453 us -> 285 us (0.63)
  waiting for transfers between devices: 354 us -> 122 us
  starting transfers between devices: 12.4 us -> 55.7 us
  other arithmetic: 6.9 us -> 29.1 us
  between operations: 14.2 us -> 1.39 us
  Pallas kernels: 49.4 us -> 57.1 us
    unnamed x3 -> x0, waiting for transfers between devices: 208 us -> none
    ppermute x0 -> x52, waiting for transfers between devices: none -> 104 us  [moved(): return lax.ppermute(value, axes, pairs)]
    all_gather x1 -> x0, waiting for transfers between devices: 68.9 us -> none  [gather_params(): return lax.all_gather(params.reshape(-1, LANES), AXES, axis=0, tiled=True)]
    all_to_all x1, waiting for transfers between devices: 53 us -> 0.01 us  [local(): lax.all_to_all(guess[rows], AXES, split_axis=0, concat_axis=0, tiled=True)]
    ppermute x0 -> x52, starting transfers between devices: none -> 44.3 us  [moved(): return lax.ppermute(value, axes, pairs)]
    add x0 -> x16, other arithmetic: none -> 20.6 us  [the longest x4 7.46 us: scatter_pieces(): p = moved(mine[0:2] + got[0:2], axes, far)]
    ppermute x1, waiting for transfers between devices: 21.5 us -> 12.8 us  [local(): low = lax.ppermute(planes(depth - 2, depth - 1), AXES, flat_ring(1))]
    pallas_call x1, Pallas kernels: 30.6 us -> 38.7 us  [learn(): pl.pallas_call(functools.partial(learn_kernel, shapes, count, len(pieces)...]
  transfers between devices with their start and end apart: 6 -> 56, of which waited for: 5 -> 19; matrix products, arithmetic and copies ran while one was open for 4% -> 15% of each run, Pallas kernels for 4% -> 6%
where the time goes in v2:
time: 285 us; the launch traced here: 284 us
  waiting for transfers between devices  122 us (43%)
  Pallas kernels  57.1 us (20%)
  starting transfers between devices  55.7 us (20%)
  other arithmetic  29.1 us (10%)
  local copies, waits for them, and re-layouts  19.6 us (7%)
    ppermute x52, waiting for transfers between devices, moved(): return lax.ppermute(value, axes, pairs)  104 us
    ppermute x52, starting transfers between devices, moved(): return lax.ppermute(value, axes, pairs)  44.3 us
    pallas_call x1, Pallas kernels, learn(): pl.pallas_call(functools.partial(learn_kernel, shapes, count, len(pieces)...  38.7 us
    pallas_call x1, Pallas kernels, physics(): pl.pallas_call(physics_kernel, name='physics', out_shape=(jax.ShapeDtypeS...  18.4 us
    ppermute x1, waiting for transfers between devices, local(): low = lax.ppermute(planes(depth - 2, depth - 1), AXES, flat_ring(1))  12.8 us
    add x4, other arithmetic, scatter_pieces(): p = moved(mine[0:2] + got[0:2], axes, far)  7.46 us
  transfers between devices with their start and end apart: 56, of which 19 were waited for; matrix products, arithmetic and copies ran while one was open for 15% of the time, Pallas kernels for 6%

profile of v2, /device:TPU:0, one launch (start us, length us, event | category | flops | bytes accessed | tf_op | source)
XLA Modules:
  0.0 284.5 jit_solution(4248352528339998591)
XLA Ops:
  5.2 4.4 %collective-permute-start = (f32[7,128,128]{2,1,0:T(8,128)}, f32[7,128,128]{2,1,0:T(8,128)S(1)}, u32[]{:S(2)}, u32[]{:S(2)}) collective-permute-start(f32[7,128,128]{2,1,0:T(8,128)} %pad_maximum_fusion), channel_id=1, source_target_pairs={{0,1},{1,2},{2,3},{3,4},{4,5},{5,6},{6,7},{7,8},{8,9},{9,10},{10,1... | collective-permute-start | bytes 1376264 | tf_op jit(solution)/shard_map/ppermute | solution.py:494
  11.8 2.7 collective-permute-start.4
  14.5 3.3 %collective-permute-start.6 = (f32[2,448,128]{2,1,0:T(8,128)S(1)}, f32[2,448,128]{2,1,0:T(8,128)S(1)}, u32[]{:S(2)}, u32[]{:S(2)}) collective-permute-start(f32[2,448,128]{2,1,0:T(8,128)S(1)} %maximum_select_fusion.refs_0_), channel_id=1, source_target_pairs={{0,16},{1,17},{2,18},{3,19},{4,20},{5,21},{6,22},{7,23},{8,9},{9,8... | collective-permute-start | bytes 1376264 | tf_op jit(solution)/shard_map/ppermute | solution.py:367
  17.9 12.8 %collective-permute-done.low = f32[7,128,128]{2,1,0:T(8,128)S(1)} collective-permute-done((f32[7,128,128]{2,1,0:T(8,128)}, f32[7,128,128]{2,1,0:T(8,128)S(1)}, u32[]{:S(2)}, u32[]{:S(2)}) %collective-permute-start) | collective-permute-done | bytes 458784 | tf_op jit(solution)/shard_map/ppermute | solution.py:494
  31.3 8.5 %collective-permute-done.4.refs_2_ = f32[2,448,128]{2,1,0:T(8,128)S(1)} collective-permute-done((f32[2,448,128]{2,1,0:T(8,128)S(1)}, f32[2,448,128]{2,1,0:T(8,128)S(1)}, u32[]{:S(2)}, u32[]{:S(2)}) %collective-permute-start.4) | collective-permute-done | bytes 458784 | tf_op jit(solution)/shard_map/ppermute | solution.py:367
  41.1 5.8 %collective-permute-start.8 = (f32[2,448,128]{2,1,0:T(8,128)S(1)}, f32[2,448,128]{2,1,0:T(8,128)S(1)}, u32[]{:S(2)}, u32[]{:S(2)}) collective-permute-start(f32[2,448,128]{2,1,0:T(8,128)S(1)} %collective-permute-done.4.refs_2_), channel_id=1, source_target_pairs={{0,16},{1,17},{2,18},{3,19},{4,20},{5,21},{6,22},{7,23},{8,9},{9,8... | collective-permute-start | bytes 1376264 | tf_op jit(solution)/shard_map/ppermute | solution.py:367
  50.1 7.7 %collective-permute-done.8.refs_6_ = f32[2,448,128]{2,1,0:T(8,128)S(1)} collective-permute-done((f32[2,448,128]{2,1,0:T(8,128)S(1)}, f32[2,448,128]{2,1,0:T(8,128)S(1)}, u32[]{:S(2)}, u32[]{:S(2)}) %collective-permute-start.8) | collective-permute-done | bytes 458784 | tf_op jit(solution)/shard_map/ppermute | solution.py:367
  59.4 3.3 %collective-permute-done.14.refs_12_ = f32[2,448,128]{2,1,0:T(8,128)S(1)} collective-permute-done((f32[2,448,128]{2,1,0:T(8,128)S(1)}, f32[2,448,128]{2,1,0:T(8,128)S(1)}, u32[]{:S(2)}, u32[]{:S(2)}) %collective-permute-start.14) | collective-permute-done | bytes 458784 | tf_op jit(solution)/shard_map/ppermute | solution.py:367
  64.5 7.8 %collective-permute-done.28 = f32[2,448,128]{2,1,0:T(8,128)S(1)} collective-permute-done((f32[2,448,128]{2,1,0:T(8,128)S(1)}, f32[2,448,128]{2,1,0:T(8,128)S(1)}, u32[]{:S(2)}, u32[]{:S(2)}) %collective-permute-start.28) | collective-permute-done | bytes 458784 | tf_op jit(solution)/shard_map/ppermute | solution.py:367
  76.4 10.0 %collective-permute-done.21.refs_18_ = f32[2,448,128]{2,1,0:T(8,128)S(1)} collective-permute-done((f32[2,448,128]{2,1,0:T(8,128)S(1)}, f32[2,448,128]{2,1,0:T(8,128)S(1)}, u32[]{:S(2)}, u32[]{:S(2)}) %collective-permute-start.21) | collective-permute-done | bytes 458784 | tf_op jit(solution)/shard_map/ppermute | solution.py:367
  89.4 3.0 %collective-permute-done.30.refs_26_ = f32[2,448,128]{2,1,0:T(8,128)} collective-permute-done((f32[2,448,128]{2,1,0:T(8,128)}, f32[2,448,128]{2,1,0:T(8,128)}, u32[]{:S(2)}, u32[]{:S(2)}) %collective-permute-start.30) | collective-permute-done | bytes 458784 | tf_op jit(solution)/shard_map/ppermute | solution.py:367
  93.8 2.4 collective-permute-done.25.refs_22_
  96.5 4.7 %collective-permute-done.32.refs_28_ = f32[2,448,128]{2,1,0:T(8,128)} collective-permute-done((f32[2,448,128]{2,1,0:T(8,128)}, f32[2,448,128]{2,1,0:T(8,128)}, u32[]{:S(2)}, u32[]{:S(2)}) %collective-permute-start.32) | collective-permute-done | bytes 458784 | tf_op jit(solution)/shard_map/ppermute | solution.py:367
  101.4 4.7 %collective-permute-done.34.refs_30_ = f32[2,448,128]{2,1,0:T(8,128)} collective-permute-done((f32[2,448,128]{2,1,0:T(8,128)}, f32[2,448,128]{2,1,0:T(8,128)}, u32[]{:S(2)}, u32[]{:S(2)}) %collective-permute-start.34) | collective-permute-done | bytes 458784 | tf_op jit(solution)/shard_map/ppermute | solution.py:367
  107.6 18.4 %physics.1 = (f32[3,8,128,128]{3,2,1,0:T(8,128)}, f32[256,1536]{1,0:T(8,128)S(1)}, f32[256,1536]{1,0:T(8,128)S(1)}) custom-call(f32[3,8,128,128]{3,2,1,0:T(8,128)S(1)} %copy-done.2, f32[7,128,128]{2,1,0:T(8,128)S(1)} %collective-permute-done.low, f32[7,128,128]{2,1,0:T(8,128)S(1)} %collective-permute-done.1.high, f32[8,128,128]{2,1,0:T(8,128)S(1)} %copy-done.3), custom_call_target="tpu_custom_call" | custom-call | flops 47185920 | bytes 6291456 | tf_op jit(solution)/shard_map/physics/pallas_call | solution.py:133
  128.3 38.7 %learn.1 = (f32[256,1536]{1,0:T(8,128)}, f32[8,448,128]{2,1,0:T(8,128)}, f32[8,448,128]{2,1,0:T(8,128)}, f32[8,448,128]{2,1,0:T(8,128)}, f32[8,448,128]{2,1,0:T(...) custom-call(s32[64]{0:T(128)} %stack.338.rows_in, ...), custom_call_target="tpu_custom_call" | custom-call | flops 16911433728 | bytes 29360128 | tf_op jit(solution)/shard_map/learn/pallas_call | solution.py:333
  168.1 3.2 %sort.17 = (s32[256]{0:T(256)}, s32[256]{0:T(256)S(1)}) sort(s32[256]{0:T(256)S(1)} %and_select_fusion.2, s32[256]{0:T(256)S(1)} %iota.7), dimensions={0}, to_apply=%region_0.1 | sort | flops 2048 | bytes 4096 | tf_op jit(solution)/shard_map/jit(argsort)/sort | solution.py:499
  174.0 3.0 %all-to-all-start.1 = ((s32[32,8,1]{1,2,0:T(1,128)}), s32[32,8,1]{1,2,0:T(1,128)S(1)}, u32[]{:S(2)}, u32[]{:S(2)}) async-start(s32[32,8,1]{1,2,0:T(1,128)} %bitcast.75), calls=%async_computation.1 | async-start | bytes 32768 | tf_op jit(solution)/shard_map/all_to_all | solution.py:503
  179.0 5.1 %all-to-all-done.1 = s32[32,8,1]{1,2,0:T(1,128)S(1)} async-done(((s32[32,8,1]{1,2,0:T(1,128)}), s32[32,8,1]{1,2,0:T(1,128)S(1)}, u32[]{:S(2)}, u32[]{:S(2)}) %all-to-all-start.1) | async-done | bytes 1056 | tf_op jit(solution)/shard_map/all_to_all | solution.py:503
  185.5 2.3 slice_add_fusion.1
  188.5 2.3 slice_add_fusion
  192.3 2.3 gather_fusion.1
  194.6 2.7 all-to-all-start
  202.3 2.7 collective-permute-done.43
  209.0 19.8 %collective-permute-done.49 = f32[2,2,448,128]{3,2,1,0:T(8,128)} collective-permute-done((f32[2,2,448,128]{3,2,1,0:T(8,128)}, f32[2,2,448,128]{3,2,1,0:T(8,128)}, u32[]{:S(2)}, u32[]{:S(2)}) %collective-permute-start.49) | collective-permute-done | bytes 917536 | tf_op jit(solution)/shard_map/ppermute | solution.py:367
  232.3 3.8 %collective-permute-start.45 = (f32[2,448,128]{2,1,0:T(8,128)S(1)}, f32[2,448,128]{2,1,0:T(8,128)S(1)}, u32[]{:S(2)}, u32[]{:S(2)}) collective-permute-start(f32[2,448,128]{2,1,0:T(8,128)S(1)} %fusion.9), channel_id=1, source_target_pairs={{0,2},{1,3},{6,4},{7,5},{8,10},{9,11},{14,12},{15,13},{16,18},{17,... | collective-permute-start | bytes 1376264 | tf_op jit(solution)/shard_map/ppermute | solution.py:367
  236.1 11.7 %collective-permute-done.40 = f32[2,2,448,128]{3,2,1,0:T(8,128)S(1)} collective-permute-done((f32[2,2,448,128]{3,2,1,0:T(8,128)S(1)}, f32[2,2,448,128]{3,2,1,0:T(8,128)S(1)}, u32[]{:S(2)}, u32[]{:S(2)}) %collective-permute-start.40) | collective-permute-done | bytes 917536 | tf_op jit(solution)/shard_map/ppermute | solution.py:367
  250.1 2.4 collective-permute-start.51
  254.0 7.3 %collective-permute-done.37 = f32[2,2,448,128]{3,2,1,0:T(8,128)S(1)} collective-permute-done((f32[2,2,448,128]{3,2,1,0:T(8,128)S(1)}, f32[2,2,448,128]{3,2,1,0:T(8,128)S(1)}, u32[]{:S(2)}, u32[]{:S(2)}) %collective-permute-start.37) | collective-permute-done | bytes 917536 | tf_op jit(solution)/shard_map/ppermute | solution.py:367
  267.8 2.6 collective-permute-start.47
  271.9 6.2 %collective-permute-done.47 = f32[2,448,128]{2,1,0:T(8,128)} collective-permute-done((f32[2,448,128]{2,1,0:T(8,128)}, f32[2,448,128]{2,1,0:T(8,128)}, u32[]{:S(2)}, u32[]{:S(2)}) %collective-permute-start.47) | collective-permute-done | bytes 458784 | tf_op jit(solution)/shard_map/ppermute | solution.py:367
  279.8 2.3 gather_fusion.3
  (208 shorter events, 64.9 us)
Async XLA Ops:
  5.2 25.5 %collective-permute-start = (f32[7,128,128]{2,1,0:T(8,128)}, f32[7,128,128]{2,1,0:T(8,128)S(1)}, u32[]{:S(2)}, u32[]{:S(2)}) collective-permute-start(f32[7,128,128]{2,1,0:T(8,128)} %pad_maximum_fusion), channel_id=1, source_target_pairs={{0,1},{1,2},{2,3},{3,4},{4,5},{5,6},{6,7},{7,8},{8,9},{9,10},{10,1... | collective-permute-start | bytes 1376264 | tf_op jit(solution)/shard_map/ppermute | solution.py:494
  10.4 20.2 %collective-permute-start.1 = (f32[7,128,128]{2,1,0:T(8,128)}, f32[7,128,128]{2,1,0:T(8,128)S(1)}, u32[]{:S(2)}, u32[]{:S(2)}) collective-permute-start(f32[7,128,128]{2,1,0:T(8,128)} %pad_maximum_fusion.1), channel_id=1, source_target_pairs={{1,0},{2,1},{3,2},{4,3},{5,4},{6,5},{7,6},{8,7},{9,8},{10,9},{11,1... | collective-permute-start | bytes 1376264 | tf_op jit(solution)/shard_map/ppermute | solution.py:495
  11.8 28.1 %collective-permute-start.4 = (f32[2,448,128]{2,1,0:T(8,128)S(1)}, f32[2,448,128]{2,1,0:T(8,128)S(1)}, u32[]{:S(2)}, u32[]{:S(2)}) collective-permute-start(f32[2,448,128]{2,1,0:T(8,128)S(1)} %maximum_select_fusion.refs_0_), channel_id=1, source_target_pairs={{0,1},{1,0},{2,3},{3,2},{4,5},{5,4},{6,7},{7,6},{8,24},{9,25},{10,... | collective-permute-start | bytes 1376264 | tf_op jit(solution)/shard_map/ppermute | solution.py:367
  14.5 25.4 %collective-permute-start.6 = (f32[2,448,128]{2,1,0:T(8,128)S(1)}, f32[2,448,128]{2,1,0:T(8,128)S(1)}, u32[]{:S(2)}, u32[]{:S(2)}) collective-permute-start(f32[2,448,128]{2,1,0:T(8,128)S(1)} %maximum_select_fusion.refs_0_), channel_id=1, source_target_pairs={{0,16},{1,17},{2,18},{3,19},{4,20},{5,21},{6,22},{7,23},{8,9},{9,8... | collective-permute-start | bytes 1376264 | tf_op jit(solution)/shard_map/ppermute | solution.py:367
  17.9 22.6 %collective-permute-start.10 = (f32[2,448,128]{2,1,0:T(8,128)S(1)}, f32[2,448,128]{2,1,0:T(8,128)S(1)}, u32[]{:S(2)}, u32[]{:S(2)}) collective-permute-start(f32[2,448,128]{2,1,0:T(8,128)S(1)} %maximum_select_fusion.refs_0_), channel_id=1, source_target_pairs={{0,2},{1,3},{2,0},{3,1},{4,6},{5,7},{6,4},{7,5},{8,10},{9,11},{10,... | collective-permute-start | bytes 1376264 | tf_op jit(solution)/shard_map/ppermute | solution.py:367
  30.6 16.3 %collective-permute-start.18 = (f32[2,448,128]{2,1,0:T(8,128)S(1)}, f32[2,448,128]{2,1,0:T(8,128)S(1)}, u32[]{:S(2)}, u32[]{:S(2)}) collective-permute-start(f32[2,448,128]{2,1,0:T(8,128)S(1)} %maximum_select_fusion.refs_0_), channel_id=1, source_target_pairs={{2,4},{3,5},{4,2},{5,3},{10,12},{11,13},{12,10},{13,11},{18,20},{1... | collective-permute-start | bytes 1376264 | tf_op jit(solution)/shard_map/ppermute | solution.py:367
  41.1 16.6 %collective-permute-start.8 = (f32[2,448,128]{2,1,0:T(8,128)S(1)}, f32[2,448,128]{2,1,0:T(8,128)S(1)}, u32[]{:S(2)}, u32[]{:S(2)}) collective-permute-start(f32[2,448,128]{2,1,0:T(8,128)S(1)} %collective-permute-done.4.refs_2_), channel_id=1, source_target_pairs={{0,16},{1,17},{2,18},{3,19},{4,20},{5,21},{6,22},{7,23},{8,9},{9,8... | collective-permute-start | bytes 1376264 | tf_op jit(solution)/shard_map/ppermute | solution.py:367
  46.9 15.7 %collective-permute-start.14 = (f32[2,448,128]{2,1,0:T(8,128)S(1)}, f32[2,448,128]{2,1,0:T(8,128)S(1)}, u32[]{:S(2)}, u32[]{:S(2)}) collective-permute-start(f32[2,448,128]{2,1,0:T(8,128)S(1)} %collective-permute-done.10.refs_8_), channel_id=1, source_target_pairs={{0,16},{1,17},{2,18},{3,19},{4,20},{5,21},{6,22},{7,23},{8,9},{9,8... | collective-permute-start | bytes 1376264 | tf_op jit(solution)/shard_map/ppermute | solution.py:367
  47.4 16.5 %collective-permute-start.19 = (f32[2,448,128]{2,1,0:T(8,128)S(1)}, f32[2,448,128]{2,1,0:T(8,128)S(1)}, u32[]{:S(2)}, u32[]{:S(2)}) collective-permute-start(f32[2,448,128]{2,1,0:T(8,128)S(1)} %collective-permute-done.18), channel_id=1, source_target_pairs={{2,0},{3,1},{4,6},{5,7},{10,8},{11,9},{12,14},{13,15},{18,16},{19,... | collective-permute-start | bytes 1376264 | tf_op jit(solution)/shard_map/ppermute | solution.py:367
  48.8 23.6 %collective-permute-start.28 = (f32[2,448,128]{2,1,0:T(8,128)S(1)}, f32[2,448,128]{2,1,0:T(8,128)S(1)}, u32[]{:S(2)}, u32[]{:S(2)}) collective-permute-start(f32[2,448,128]{2,1,0:T(8,128)S(1)} %collective-permute-done.27), channel_id=1, source_target_pairs={{2,0},{3,1},{4,6},{5,7},{10,8},{11,9},{12,14},{13,15},{18,16},{19,... | collective-permute-start | bytes 1376264 | tf_op jit(solution)/shard_map/ppermute | solution.py:367
  57.8 15.6 %collective-permute-start.11 = (f32[2,448,128]{2,1,0:T(8,128)S(1)}, f32[2,448,128]{2,1,0:T(8,128)S(1)}, u32[]{:S(2)}, u32[]{:S(2)}) collective-permute-start(f32[2,448,128]{2,1,0:T(8,128)S(1)} %collective-permute-done.10.refs_8_), channel_id=1, source_target_pairs={{0,8},{1,9},{2,10},{3,11},{4,12},{5,13},{6,14},{7,15},{8,0},{9,1},... | collective-permute-start | bytes 1376264 | tf_op jit(solution)/shard_map/ppermute | solution.py:367
  59.4 14.4 %collective-permute-start.9 = (f32[2,448,128]{2,1,0:T(8,128)S(1)}, f32[2,448,128]{2,1,0:T(8,128)S(1)}, u32[]{:S(2)}, u32[]{:S(2)}) collective-permute-start(f32[2,448,128]{2,1,0:T(8,128)S(1)} %collective-permute-done.8.refs_6_), channel_id=1, source_target_pairs={{0,8},{1,9},{2,10},{3,11},{4,12},{5,13},{6,14},{7,15},{8,0},{9,1},... | collective-permute-start | bytes 1376264 | tf_op jit(solution)/shard_map/ppermute | solution.py:367
  74.6 13.7 %collective-permute-start.17 = (f32[2,448,128]{2,1,0:T(8,128)S(1)}, f32[2,448,128]{2,1,0:T(8,128)S(1)}, u32[]{:S(2)}, u32[]{:S(2)}) collective-permute-start(f32[2,448,128]{2,1,0:T(8,128)S(1)} %collective-permute-done.16.refs_14_), channel_id=1, source_target_pairs={{0,8},{1,9},{2,10},{3,11},{4,12},{5,13},{6,14},{7,15},{8,0},{9,1},... | collective-permute-start | bytes 1376264 | tf_op jit(solution)/shard_map/ppermute | solution.py:367
  75.1 17.3 %collective-permute-start.30 = (f32[2,448,128]{2,1,0:T(8,128)}, f32[2,448,128]{2,1,0:T(8,128)}, u32[]{:S(2)}, u32[]{:S(2)}) collective-permute-start(f32[2,448,128]{2,1,0:T(8,128)} %add.728.refs_24_), channel_id=1, source_target_pairs={{0,1},{1,0},{2,3},{3,2},{4,5},{5,4},{6,7},{7,6},{8,24},{9,25},{10,... | collective-permute-start | bytes 1376264 | tf_op jit(solution)/shard_map/ppermute | solution.py:367
  92.4 13.7 %collective-permute-start.34 = (f32[2,448,128]{2,1,0:T(8,128)}, f32[2,448,128]{2,1,0:T(8,128)}, u32[]{:S(2)}, u32[]{:S(2)}) collective-permute-start(f32[2,448,128]{2,1,0:T(8,128)} %collective-permute-done.30.refs_26_), channel_id=1, source_target_pairs={{0,16},{1,17},{2,18},{3,19},{4,20},{5,21},{6,22},{7,23},{8,9},{9,8... | collective-permute-start | bytes 1376264 | tf_op jit(solution)/shard_map/ppermute | solution.py:367
  93.2 35.1 %collective-permute-start.29 = (f32[2,448,128]{2,1,0:T(8,128)}, f32[2,448,128]{2,1,0:T(8,128)}, u32[]{:S(2)}, u32[]{:S(2)}) collective-permute-start(f32[2,448,128]{2,1,0:T(8,128)} %add.728.refs_24_), channel_id=1, source_target_pairs={{0,8},{1,9},{2,10},{3,11},{4,12},{5,13},{6,14},{7,15},{8,0},{9,1},... | collective-permute-start | bytes 1376264 | tf_op jit(solution)/shard_map/ppermute | solution.py:367
  93.3 35.0 %collective-permute-start.31 = (f32[2,448,128]{2,1,0:T(8,128)}, f32[2,448,128]{2,1,0:T(8,128)}, u32[]{:S(2)}, u32[]{:S(2)}) collective-permute-start(f32[2,448,128]{2,1,0:T(8,128)} %collective-permute-done.30.refs_26_), channel_id=1, source_target_pairs={{0,8},{1,9},{2,10},{3,11},{4,12},{5,13},{6,14},{7,15},{8,0},{9,1},... | collective-permute-start | bytes 1376264 | tf_op jit(solution)/shard_map/ppermute | solution.py:367
  96.2 32.0 %collective-permute-start.26 = (f32[2,448,128]{2,1,0:T(8,128)}, f32[2,448,128]{2,1,0:T(8,128)}, u32[]{:S(2)}, u32[]{:S(2)}) collective-permute-start(f32[2,448,128]{2,1,0:T(8,128)} %collective-permute-done.25.refs_22_), channel_id=1, source_target_pairs={{0,8},{1,9},{2,10},{3,11},{4,12},{5,13},{6,14},{7,15},{8,0},{9,1},... | collective-permute-start | bytes 1376264 | tf_op jit(solution)/shard_map/ppermute | solution.py:367
  101.2 27.1 %collective-permute-start.33 = (f32[2,448,128]{2,1,0:T(8,128)}, f32[2,448,128]{2,1,0:T(8,128)}, u32[]{:S(2)}, u32[]{:S(2)}) collective-permute-start(f32[2,448,128]{2,1,0:T(8,128)} %collective-permute-done.32.refs_28_), channel_id=1, source_target_pairs={{0,8},{1,9},{2,10},{3,11},{4,12},{5,13},{6,14},{7,15},{8,0},{9,1},... | collective-permute-start | bytes 1376264 | tf_op jit(solution)/shard_map/ppermute | solution.py:367
  106.1 22.2 %collective-permute-start.35 = (f32[2,448,128]{2,1,0:T(8,128)}, f32[2,448,128]{2,1,0:T(8,128)}, u32[]{:S(2)}, u32[]{:S(2)}) collective-permute-start(f32[2,448,128]{2,1,0:T(8,128)} %collective-permute-done.34.refs_30_), channel_id=1, source_target_pairs={{0,8},{1,9},{2,10},{3,11},{4,12},{5,13},{6,14},{7,15},{8,0},{9,1},... | collective-permute-start | bytes 1376264 | tf_op jit(solution)/shard_map/ppermute | solution.py:367
  167.1 18.4 %collective-permute-start.42 = (f32[4,2,448,128]{3,2,1,0:T(8,128)}, f32[4,2,448,128]{3,2,1,0:T(8,128)}, u32[]{:S(2)}, u32[]{:S(2)}) collective-permute-start(f32[4,2,448,128]{3,2,1,0:T(8,128)} %bitcast.212), channel_id=1, source_target_pairs={{0,8},{1,9},{2,10},{3,11},{4,12},{5,13},{6,14},{7,15},{8,0},{9,1},... | collective-permute-start | bytes 5505032 | tf_op jit(solution)/shard_map/ppermute | solution.py:367
  167.5 21.0 %collective-permute-start.48 = (f32[4,2,448,128]{3,2,1,0:T(8,128)}, f32[4,2,448,128]{3,2,1,0:T(8,128)}, u32[]{:S(2)}, u32[]{:S(2)}) collective-permute-start(f32[4,2,448,128]{3,2,1,0:T(8,128)} %bitcast.211), channel_id=1, source_target_pairs={{0,8},{1,9},{2,10},{3,11},{4,12},{5,13},{6,14},{7,15},{8,0},{9,1},... | collective-permute-start | bytes 5505032 | tf_op jit(solution)/shard_map/ppermute | solution.py:367
  167.6 31.5 %collective-permute-start.39 = (f32[4,2,448,128]{3,2,1,0:T(8,128)}, f32[4,2,448,128]{3,2,1,0:T(8,128)}, u32[]{:S(2)}, u32[]{:S(2)}) collective-permute-start(f32[4,2,448,128]{3,2,1,0:T(8,128)} %bitcast.210), channel_id=1, source_target_pairs={{0,8},{1,9},{2,10},{3,11},{4,12},{5,13},{6,14},{7,15},{8,0},{9,1},... | collective-permute-start | bytes 5505032 | tf_op jit(solution)/shard_map/ppermute | solution.py:367
  171.2 35.1 %collective-permute-start.36 = (f32[4,2,448,128]{3,2,1,0:T(8,128)}, f32[4,2,448,128]{3,2,1,0:T(8,128)}, u32[]{:S(2)}, u32[]{:S(2)}) collective-permute-start(f32[4,2,448,128]{3,2,1,0:T(8,128)} %bitcast.209), channel_id=1, source_target_pairs={{0,8},{1,9},{2,10},{3,11},{4,12},{5,13},{6,14},{7,15},{8,0},{9,1},... | collective-permute-start | bytes 5505032 | tf_op jit(solution)/shard_map/ppermute | solution.py:367
  187.8 17.2 %collective-permute-start.43 = (f32[2,2,448,128]{3,2,1,0:T(8,128)}, f32[2,2,448,128]{3,2,1,0:T(8,128)}, u32[]{:S(2)}, u32[]{:S(2)}) collective-permute-start(f32[2,2,448,128]{3,2,1,0:T(8,128)} %slice_add_fusion.1), channel_id=1, source_target_pairs={{0,16},{1,17},{2,18},{3,19},{4,20},{5,21},{6,22},{7,23},{8,9},{9,8... | collective-permute-start | bytes 2752520 | tf_op jit(solution)/shard_map/ppermute | solution.py:367
  190.8 38.0 %collective-permute-start.49 = (f32[2,2,448,128]{3,2,1,0:T(8,128)}, f32[2,2,448,128]{3,2,1,0:T(8,128)}, u32[]{:S(2)}, u32[]{:S(2)}) collective-permute-start(f32[2,2,448,128]{3,2,1,0:T(8,128)} %slice_add_fusion), channel_id=1, source_target_pairs={{0,16},{1,17},{2,18},{3,19},{4,20},{5,21},{6,22},{7,23},{8,9},{9,8... | collective-permute-start | bytes 2752520 | tf_op jit(solution)/shard_map/ppermute | solution.py:367
  194.6 85.2 %all-to-all-start = ((f32[32,8,1536]{2,1,0:T(8,128)}), f32[32,8,1536]{2,1,0:T(8,128)S(1)}, u32[]{:S(2)}, u32[]{:S(2)}) async-start(f32[32,8,1536]{2,1,0:T(8,128)} %bitcast.197), calls=%async_computation | async-start | bytes 3145728 | tf_op jit(solution)/shard_map/all_to_all | solution.py:510
  200.6 47.2 %collective-permute-start.40 = (f32[2,2,448,128]{3,2,1,0:T(8,128)S(1)}, f32[2,2,448,128]{3,2,1,0:T(8,128)S(1)}, u32[]{:S(2)}, u32[]{:S(2)}) collective-permute-start(f32[2,2,448,128]{3,2,1,0:T(8,128)S(1)} %slice_add_fusion.2), channel_id=1, source_target_pairs={{0,16},{1,17},{2,18},{3,19},{4,20},{5,21},{6,22},{7,23},{8,9},{9,8... | collective-permute-start | bytes 2752520 | tf_op jit(solution)/shard_map/ppermute | solution.py:367
  206.2 24.8 %collective-permute-start.44 = (f32[2,448,128]{2,1,0:T(8,128)S(1)}, f32[2,448,128]{2,1,0:T(8,128)S(1)}, u32[]{:S(2)}, u32[]{:S(2)}) collective-permute-start(f32[2,448,128]{2,1,0:T(8,128)S(1)} %fusion.6), channel_id=1, source_target_pairs={{0,1},{1,0},{2,3},{3,2},{4,5},{5,4},{6,7},{7,6},{8,24},{9,25},{10,... | collective-permute-start | bytes 1376264 | tf_op jit(solution)/shard_map/ppermute | solution.py:367
  207.7 53.6 %collective-permute-start.37 = (f32[2,2,448,128]{3,2,1,0:T(8,128)S(1)}, f32[2,2,448,128]{3,2,1,0:T(8,128)S(1)}, u32[]{:S(2)}, u32[]{:S(2)}) collective-permute-start(f32[2,2,448,128]{3,2,1,0:T(8,128)S(1)} %slice_add_fusion.3), channel_id=1, source_target_pairs={{0,16},{1,17},{2,18},{3,19},{4,20},{5,21},{6,22},{7,23},{8,9},{9,8... | collective-permute-start | bytes 2752520 | tf_op jit(solution)/shard_map/ppermute | solution.py:367
  230.1 18.8 %collective-permute-start.50 = (f32[2,448,128]{2,1,0:T(8,128)S(1)}, f32[2,448,128]{2,1,0:T(8,128)S(1)}, u32[]{:S(2)}, u32[]{:S(2)}) collective-permute-start(f32[2,448,128]{2,1,0:T(8,128)S(1)} %fusion.1), channel_id=1, source_target_pairs={{0,1},{1,0},{2,3},{3,2},{4,5},{5,4},{6,7},{7,6},{8,24},{9,25},{10,... | collective-permute-start | bytes 1376264 | tf_op jit(solution)/shard_map/ppermute | solution.py:367
  232.3 21.0 %collective-permute-start.45 = (f32[2,448,128]{2,1,0:T(8,128)S(1)}, f32[2,448,128]{2,1,0:T(8,128)S(1)}, u32[]{:S(2)}, u32[]{:S(2)}) collective-permute-start(f32[2,448,128]{2,1,0:T(8,128)S(1)} %fusion.9), channel_id=1, source_target_pairs={{0,2},{1,3},{6,4},{7,5},{8,10},{9,11},{14,12},{15,13},{16,18},{17,... | collective-permute-start | bytes 1376264 | tf_op jit(solution)/shard_map/ppermute | solution.py:367
  (62 other events, 1153.2 us)
